TPU v7x, 32 devices: a whole 2x2x4 slice. The times are simulated.
32 devices in a mesh: row: 4 (over y, core), col: 8 (over z, x).
Axes of the slice: x: 2, y: 2, z: 4, core: 2. Of those that a mesh axis runs over, the one named last changes fastest.
Arguments:
- rhs: float32 [8, 8192], P(None, ('row', 'col')), may hold values from -6 to 6
- stiff_diag: float32 [8192], P(('row', 'col')), may hold values from 1 to 4
- tiles: bfloat16 [4, 8, 8, 128, 128], P('row', 'col'), may hold values from -0.15625 to 0.15625
- tile_cols: int32 [4, 8, 8], P('row', 'col'), may hold values from 0 to 7
- tile_offsets: int32 [4, 8, 8], P('row', 'col'), may hold values from 0 to 1, as said below
- tile_counts: int32 [4, 8, 1], P('row', 'col'), may hold values from 4 to 8, as said below
Outputs:
- solution: float32 [8, 8192], P(None, ('row', 'col'))
- residual: float32 [8, 8192], P(None, ('row', 'col'))
Inputs may be any that keep to these rules, and one draw needn't show every extreme that they name: `tile_offsets`: within one grid cell, slots t with the same t mod 8 carry different offsets. `tile_counts`: some grid cell has all 8 slots live.
All inputs are finite; a program needn't handle non-finite values.
Results may differ from a plain program's by a relative error of at most 0.0035.
Values may be sent and summed in bfloat16 or wider, within the bound.
No kernel may reach another device: no remote copies, remote signals or barrier semaphores. Data moves between devices by JAX's collectives and lax.ppermute only.
A program may use at most 64 MiB of HBM per device.

v0:
```python
import jax
import jax.numpy as jnp
from jax import lax
from jax.sharding import PartitionSpec as P

STEPS = 3


lower_bound = 0.3
upper_bound = 1.9


def body(rhs, stiff_diag, tiles, tile_cols, tile_offsets, tile_counts):
    tile_set = tiles[0, 0]
    cols = tile_cols[0, 0]
    offsets = tile_offsets[0, 0]
    count = tile_counts[0, 0, 0]
    slots = tile_set.shape[0]
    width = tile_set.shape[1]
    ncol = lax.axis_size("col")
    share = slots // ncol
    piece = stiff_diag.shape[0] // width
    samples = rhs.shape[0]
    slot_ids = jnp.arange(slots, dtype=jnp.int32)
    live = (slot_ids < count).astype(jnp.float32)
    arrived = lax.all_to_all(
        offsets.reshape(share, ncol), "col", split_axis=1, concat_axis=1, tiled=True
    )
    chooser = (arrived[None, :, :] == jnp.arange(piece, dtype=jnp.int32)[:, None, None]).astype(
        jnp.float32
    )
    theta = (upper_bound + lower_bound) / 2.0
    delta = (upper_bound - lower_bound) / 2.0
    sigma = theta / delta
    inverse = 1.0 / stiff_diag
    solution = jnp.zeros_like(rhs)
    residual = rhs
    rho = 1.0 / sigma
    direction = 1.0 / theta * inverse[None, :] * residual
    for step in range(STEPS):
        solution = solution + direction
        rounded = direction.astype(jnp.bfloat16)
        gathered = lax.all_gather(rounded, "row", axis=1, tiled=True)
        blocks = gathered.reshape(samples, -1, width)
        picked = jnp.take(blocks, cols, axis=1)
        terms = jnp.einsum("tij,stj->sti", tile_set, picked, preferred_element_type=jnp.float32)
        terms = terms * live[None, :, None]
        grouped = terms.reshape(samples, share, ncol, width)
        moved = lax.all_to_all(grouped, "col", split_axis=2, concat_axis=2, tiled=True)
        summed = jnp.einsum("kan,sani->ski", chooser, moved, precision=lax.Precision.HIGHEST)
        coupled = summed.reshape(samples, piece * width)
        residual = residual - (stiff_diag[None, :] * direction + coupled)
        if step + 1 < STEPS:
            rho_new = 1.0 / (2.0 * sigma - rho)
            direction = (
                rho_new * rho * direction + 2.0 * rho_new / delta * inverse[None, :] * residual
            )
            rho = rho_new
    return (solution, residual)


def solution(mesh):
    in_specs = (
        P(None, ("row", "col")),
        P(("row", "col")),
        P("row", "col", None, None, None),
        P("row", "col", None),
        P("row", "col", None),
        P("row", "col", None),
    )
    out_specs = (P(None, ("row", "col")), P(None, ("row", "col")))
    return jax.shard_map(body, mesh=mesh, in_specs=in_specs, out_specs=out_specs, check_vma=False)
```

profile of v0, /device:TPU:0, one launch (start us, length us, event | category | flops | bytes accessed | tf_op | source)
XLA Modules:
  0.0 61.4 jit_solution(2521207246478012200)
XLA Ops:
  0.6 0.0 copy-start
  0.6 0.0 copy-start.3
  0.7 0.7 %copy-done.3 = s32[1,1,8]{2,1,0:T(1,128)S(1)} copy-done((s32[1,1,8]{2,1,0:T(1,128)S(1)}, s32[1,1,8]{2,1,0:T(1,128)}, u32[]{:S(2)}) %copy-start.3) | copy-done | bytes 56
  1.3 0.7 %copy.20 = s32[1,8,1]{2,0,1:T(1,128)} copy(s32[1,8,1]{1,2,0:T(1,128)S(1)} %bitcast.112) | data formatting | bytes 64 | tf_op jit(solution)/shard_map/all_to_all | solution.py:26
  2.0 7.3 %all-to-all-start.1 = ((s32[1,8,1]{2,0,1:T(1,128)}), s32[1,8,1]{2,0,1:T(1,128)S(1)}, u32[]{:S(2)}, u32[]{:S(2)}) async-start(s32[1,8,1]{2,0,1:T(1,128)} %copy.20), calls=%async_computation.1 | async-start | bytes 8192 | tf_op jit(solution)/shard_map/all_to_all | solution.py:26
  9.3 0.0 copy-start.4
  10.0 0.0 copy-done.4
  10.0 0.0 copy-start.2
  10.0 0.0 copy-start.1
  10.0 0.6 %copy-done.2 = f32[256]{0:T(256)S(1)} copy-done((f32[256]{0:T(256)S(1)}, f32[256]{0:T(256)}, u32[]{:S(2)}) %copy-start.2) | copy-done | bytes 1048
  10.7 0.0 copy-done.1
  10.7 5.2 %all_gather.9 = bf16[8,1024]{1,0:T(8,128)(2,1)S(1)} all-gather(bf16[8,256]{1,0:T(8,128)(2,1)S(1)} %multiply_convert_fusion), channel_id=1, replica_groups=mesh['row'=4,'col'=8] {'row'}, dimensions={1}, use_global_device_ids=true | all-gather | bytes 20480 | tf_op jit(solution)/shard_map/all_gather | solution.py:43
  15.9 0.6 gather_fusion
  16.5 0.0 copy-done
  16.5 0.9 %fusion.2 = f32[8,1,8,128]{3,0,1,2:T(8,128)} fusion(bf16[1,1,8,128,128]{4,3,2,1,0:T(8,128)(2,1)S(1)} %copy-done, bf16[8,8,128]{2,1,0:T(8,128)(2,1)S(1)} %gather_fusion, f32[8]{0:T(128)S(1)} %get-tuple-element.10, pred[8]{0:T(512)(128)(4,1)S(1)} %get-tuple-element.9), kind=kOutput, calls=%fused_computation.8 | convolution fusion | flops 2113536 | bytes 311336 | tf_op jit(solution)/shard_map/tij,stj->sti/dot_general | solution.py:46
  17.4 0.0 all-to-all-done.1
  17.4 6.0 %all-to-all-start = ((f32[8,1,8,128]{3,0,1,2:T(8,128)}), f32[8,1,8,128]{3,0,1,2:T(8,128)S(1)}, u32[]{:S(2)}, u32[]{:S(2)}) async-start(f32[8,1,8,128]{3,0,1,2:T(8,128)} %fusion.2), calls=%async_computation | async-start | bytes 65536 | tf_op jit(solution)/shard_map/all_to_all | solution.py:49
  23.4 0.2 reduce
  23.6 6.5 %all-to-all-done = f32[8,1,8,128]{3,0,1,2:T(8,128)S(1)} async-done(((f32[8,1,8,128]{3,0,1,2:T(8,128)}), f32[8,1,8,128]{3,0,1,2:T(8,128)S(1)}, u32[]{:S(2)}, u32[]{:S(2)}) %all-to-all-start) | async-done | bytes 32800 | tf_op jit(solution)/shard_map/all_to_all | solution.py:49
  30.1 0.1 convolution_bitcast_fusion.2
  30.2 5.2 %all_gather.10 = bf16[8,1024]{1,0:T(8,128)(2,1)S(1)} all-gather(bf16[8,256]{1,0:T(8,128)(2,1)S(1)} %fusion.37), channel_id=1, replica_groups=mesh['row'=4,'col'=8] {'row'}, dimensions={1}, use_global_device_ids=true | all-gather | bytes 20480 | tf_op jit(solution)/shard_map/all_gather | solution.py:43
  35.4 0.6 gather_fusion.1
  36.0 0.3 fusion.1
  36.3 9.1 %all_to_all.24 = f32[8,1,8,128]{3,0,1,2:T(8,128)S(1)} all-to-all(f32[8,1,8,128]{3,0,1,2:T(8,128)S(1)} %fusion.1), channel_id=1, replica_groups=mesh['row'=4,'col'=8] {'col'}, dimensions={2} | all-to-all | bytes 65536 | tf_op jit(solution)/shard_map/all_to_all | solution.py:49
  45.4 0.1 convolution_bitcast_fusion.1
  45.5 5.2 %all_gather.11 = bf16[8,1024]{1,0:T(8,128)(2,1)S(1)} all-gather(bf16[8,256]{1,0:T(8,128)(2,1)S(1)} %fusion.27), channel_id=1, replica_groups=mesh['row'=4,'col'=8] {'row'}, dimensions={1}, use_global_device_ids=true | all-gather | bytes 20480 | tf_op jit(solution)/shard_map/all_gather | solution.py:43
  50.7 0.6 gather_fusion.2
  51.3 0.3 fusion
  51.6 9.1 %all_to_all.25 = f32[8,1,8,128]{3,0,1,2:T(8,128)S(1)} all-to-all(f32[8,1,8,128]{3,0,1,2:T(8,128)S(1)} %fusion), channel_id=1, replica_groups=mesh['row'=4,'col'=8] {'col'}, dimensions={2} | all-to-all | bytes 65536 | tf_op jit(solution)/shard_map/all_to_all | solution.py:49
  60.6 0.1 convolution_bitcast_fusion
  60.8 0.6 %fusion.21 = (f32[8,256]{1,0:T(8,128)}, f32[8,256]{1,0:T(8,128)}) fusion(f32[1,8,2,128]{3,2,1,0:T(2,128)S(1)} %convolution_bitcast_fusion, f32[256]{0:T(256)S(1)} %get-tuple-element.8, f32[256]{0:T(256)S(1)} %copy-done.2, f32[8,256]{1,0:T(8,128)S(1)} %copy-done.1, f32[1,8,2,128]{3,2,1,0:T(2,128)S(1)} %convolution_bitcast_fusion.2, ...), kind=kLoop, calls=%fused_computation.31 | loop fusion | flops 36864 | bytes 53248 | tf_op jit(solution)/shard_map/sub | solution.py:52
  (8 shorter events, 0.1 us)
Async XLA Ops:
  0.6 15.9 %copy-start = (bf16[1,1,8,128,128]{4,3,2,1,0:T(8,128)(2,1)S(1)}, bf16[1,1,8,128,128]{4,3,2,1,0:T(8,128)(2,1)}, u32[]{:S(2)}) copy-start(bf16[1,1,8,128,128]{4,3,2,1,0:T(8,128)(2,1)} %param.10) | copy-start | bytes 786436
  0.6 0.7 %copy-start.3 = (s32[1,1,8]{2,1,0:T(1,128)S(1)}, s32[1,1,8]{2,1,0:T(1,128)}, u32[]{:S(2)}) copy-start(s32[1,1,8]{2,1,0:T(1,128)} %param.12) | copy-start | bytes 100
  2.0 15.4 %all-to-all-start.1 = ((s32[1,8,1]{2,0,1:T(1,128)}), s32[1,8,1]{2,0,1:T(1,128)S(1)}, u32[]{:S(2)}, u32[]{:S(2)}) async-start(s32[1,8,1]{2,0,1:T(1,128)} %copy.20), calls=%async_computation.1 | async-start | bytes 8192 | tf_op jit(solution)/shard_map/all_to_all | solution.py:26
  9.3 0.7 %copy-start.4 = (s32[1,1,8]{2,1,0:T(1,128)S(1)}, s32[1,1,8]{2,1,0:T(1,128)}, u32[]{:S(2)}) copy-start(s32[1,1,8]{2,1,0:T(1,128)} %param.11) | copy-start | bytes 100
  10.0 0.7 %copy-start.2 = (f32[256]{0:T(256)S(1)}, f32[256]{0:T(256)}, u32[]{:S(2)}) copy-start(f32[256]{0:T(256)} %param.9) | copy-start | bytes 3076
  10.0 0.7 %copy-start.1 = (f32[8,256]{1,0:T(8,128)S(1)}, f32[8,256]{1,0:T(8,128)}, u32[]{:S(2)}) copy-start(f32[8,256]{1,0:T(8,128)} %param.8) | copy-start | bytes 24580
  17.4 12.7 %all-to-all-start = ((f32[8,1,8,128]{3,0,1,2:T(8,128)}), f32[8,1,8,128]{3,0,1,2:T(8,128)S(1)}, u32[]{:S(2)}, u32[]{:S(2)}) async-start(f32[8,1,8,128]{3,0,1,2:T(8,128)} %fusion.2), calls=%async_computation | async-start | bytes 65536 | tf_op jit(solution)/shard_map/all_to_all | solution.py:49
where the time goes:
time: 61.8 us; the launch traced here: 61.4 us
  blocking collectives  33.8 us (55%)
  starting transfers between devices  13.3 us (22%)
  waiting for transfers between devices  6.45 us (10%)
  local copies, waits for them, and re-layouts  3.73 us (6%)
  matrix products  1.85 us (3%)
  between operations  1.4 us (2%)
  other arithmetic  0.92 us (1%)
    all_to_all x2, blocking collectives, body(): lax.all_to_all(grouped, 'col', split_axis=2, concat_axis=2, tiled=True)  18.2 us
    all_gather x3, blocking collectives, body(): gathered = lax.all_gather(rounded, 'row', axis=1, tiled=True)  15.6 us
    all_to_all x1, starting transfers between devices, body(): lax.all_to_all(offsets.reshape(share, ncol), 'col', split_axis=1, concat_...  7.28 us
    all_to_all x1, waiting for transfers between devices, body(): lax.all_to_all(grouped, 'col', split_axis=2, concat_axis=2, tiled=True)  6.45 us
    all_to_all x1, starting transfers between devices, body(): lax.all_to_all(grouped, 'col', split_axis=2, concat_axis=2, tiled=True)  6 us
    gather x3, local copies, waits for them, and re-layouts, body(): picked = jnp.take(blocks, cols, axis=1)  1.69 us
    dot_general x3, matrix products, body(): jnp.einsum('tij,stj->sti', tile_set, picked, preferred_element_type=jnp.f...  1.44 us
    unnamed x10, local copies, waits for them, and re-layouts  1.37 us
  transfers between devices with their start and end apart: 2, of which 1 were waited for; matrix products, arithmetic and copies ran while one was open for 3% of the time, Pallas kernels for 0%

commit v1 on v0

v1 whole, which is shorter than its diff:
```python
import functools

import jax
import jax.numpy as jnp
from jax import lax
from jax.experimental import pallas as pl
from jax.experimental.pallas import tpu as pltpu
from jax.sharding import PartitionSpec as P

STEPS = 3
VMEM_BYTES = 16 << 20

lower_bound = 0.3
upper_bound = 1.9

theta = (upper_bound + lower_bound) / 2.0
delta = (upper_bound - lower_bound) / 2.0
sigma = theta / delta


def coefficients():
    rho = 1.0 / sigma
    out = []
    for _ in range(STEPS - 1):
        rho_new = 1.0 / (2.0 * sigma - rho)
        out.append((rho_new * rho, 2.0 * rho_new / delta))
        rho = rho_new
    return out


def multiply(rounded, tiles, cols, count, out, rows, ncol, offsets=None):
    slots = tiles.shape[0]
    samples = rounded.shape[1]
    for t in range(slots):
        picked = rounded[cols[t]]
        prod = lax.dot_general(
            picked, tiles[t], (((1,), (1,)), ((), ())), preferred_element_type=jnp.float32
        )
        sent = jnp.where(t < count, prod, 0.0).astype(jnp.bfloat16)
        first = (t // ncol) * samples
        for r in range(rows):
            out[r * ncol + t % ncol, pl.ds(first, samples), :] = sent
            if offsets is not None:
                half = (slots // ncol) * samples
                out[r * ncol + t % ncol, pl.ds(half + first, samples), :] = jnp.full(
                    sent.shape, offsets[t], jnp.int32
                ).astype(jnp.float32).astype(jnp.bfloat16)


def part(packed, r, k, width):
    samples = packed.shape[1] - 1
    rhs = packed[r, :samples, k * width : (k + 1) * width]
    diag = packed[r, samples : samples + 1, k * width : (k + 1) * width]
    return rhs, diag


def coupled(moved, where, r, ncol, share, samples):
    def image(k):
        total = None
        for c in range(ncol):
            for a in range(share):
                piece = moved[r * ncol + c, pl.ds(a * samples, samples), :].astype(jnp.float32)
                off = where[r * ncol + c, pl.ds((share + a) * samples, samples), :]
                off = off.astype(jnp.float32)
                term = jnp.where(off == k, piece, 0.0)
                total = term if total is None else total + term
        return total

    return image


def first_kernel(dims, cols, offsets, count, packed, tiles, out, rounded):
    rows, ncol, piece, width = dims
    for r in range(rows):
        for k in range(piece):
            rhs, diag = part(packed, r, k, width)
            rounded[r * piece + k] = ((1.0 / theta) * (1.0 / diag) * rhs).astype(jnp.bfloat16)
    multiply(rounded, tiles, cols, count[0], out, rows, ncol, offsets)


def middle_kernel(dims, step, cols, count, packed, tiles, where, moved, *refs):
    rows, ncol, piece, width = dims
    samples = packed.shape[1] - 1
    share = tiles.shape[0] // ncol
    a, b = coefficients()[step]
    if step == 0:
        out, new_dir, new_res, new_sol, rounded = refs
    else:
        old_dir, old_res, old_sol, out, new_dir, new_res, new_sol, rounded = refs
    for r in range(rows):
        image = coupled(moved, where, r, ncol, share, samples)
        for k in range(piece):
            rhs, diag = part(packed, r, k, width)
            inverse = 1.0 / diag
            i = r * piece + k
            if step == 0:
                direction = (1.0 / theta) * inverse * rhs
                residual = rhs
                total = direction
            else:
                direction, residual, total = old_dir[i], old_res[i], old_sol[i]
            residual = residual - (diag * direction + image(k))
            direction = a * direction + b * inverse * residual
            new_dir[i] = direction
            new_res[i] = residual
            new_sol[i] = total + direction
            rounded[i] = direction.astype(jnp.bfloat16)
    multiply(rounded, tiles, cols, count[0], out, rows, ncol)


def last_kernel(dims, share, packed, where, moved, old_dir, old_res, old_sol, solution, residual):
    rows, ncol, piece, width = dims
    samples = packed.shape[1] - 1
    me = lax.axis_index("row")
    image = coupled(moved, where, me, ncol, share, samples)
    for k in range(piece):
        lanes = slice(k * width, (k + 1) * width)
        diag = packed[me, samples : samples + 1, lanes]
        i = me * piece + k
        solution[:, lanes] = old_sol[i]
        residual[:, lanes] = old_res[i] - (diag * old_dir[i] + image(k))


def body(rhs, stiff_diag, tiles, tile_cols, tile_offsets, tile_counts):
    tile_set = tiles[0, 0]
    cols = tile_cols[0, 0]
    offsets = tile_offsets[0, 0]
    count = tile_counts[0, 0]
    slots, width = tile_set.shape[:2]
    rows, ncol = lax.axis_size("row"), lax.axis_size("col")
    share = slots // ncol
    piece = stiff_diag.shape[0] // width
    samples = rhs.shape[0]
    blocks = rows * piece
    dims = (rows, ncol, piece, width)
    smem = pl.BlockSpec(memory_space=pltpu.SMEM)
    vmem = pl.BlockSpec(memory_space=pltpu.VMEM)
    state = jax.ShapeDtypeStruct((blocks, samples, width), jnp.float32)
    message = jax.ShapeDtypeStruct((rows * ncol, share * samples, width), jnp.bfloat16)
    wide = jax.ShapeDtypeStruct((rows * ncol, 2 * share * samples, width), jnp.bfloat16)
    scratch = [pltpu.VMEM((blocks, samples, width), jnp.bfloat16)]

    params = pltpu.CompilerParams(vmem_limit_bytes=VMEM_BYTES)

    def exchange(x):
        return lax.all_to_all(x, ("row", "col"), split_axis=0, concat_axis=0, tiled=True)

    packed = lax.all_gather(jnp.concatenate([rhs, stiff_diag[None, :]], axis=0), "row", axis=0)
    sent = pl.pallas_call(
        functools.partial(first_kernel, dims),
        out_shape=wide,
        in_specs=[smem] * 3 + [vmem] * 2,
        out_specs=vmem,
        scratch_shapes=scratch,
        compiler_params=params,
    )(cols, offsets, count, packed, tile_set)
    moved = exchange(sent)
    where = moved
    states = ()
    for step in range(STEPS - 1):
        sent, *states = pl.pallas_call(
            functools.partial(middle_kernel, dims, step),
            out_shape=(message, state, state, state),
            in_specs=[smem] * 2 + [vmem] * (4 + len(states)),
            out_specs=(vmem,) * 4,
            scratch_shapes=scratch,
            compiler_params=params,
        )(cols, count, packed, tile_set, where, moved, *states)
        moved = exchange(sent)
    out = jax.ShapeDtypeStruct(rhs.shape, jnp.float32)
    return pl.pallas_call(
        functools.partial(last_kernel, dims, share),
        out_shape=(out, out),
        in_specs=[vmem] * (3 + len(states)),
        out_specs=(vmem, vmem),
        compiler_params=params,
    )(packed, where, moved, *states)


def solution(mesh):
    in_specs = (
        P(None, ("row", "col")),
        P(("row", "col")),
        P("row", "col", None, None, None),
        P("row", "col", None),
        P("row", "col", None),
        P("row", "col", None),
    )
    out_specs = (P(None, ("row", "col")), P(None, ("row", "col")))
    return jax.shard_map(body, mesh=mesh, in_specs=in_specs, out_specs=out_specs, check_vma=False)
```

time: 61.8 us -> 46.2 us (0.75)
  starting transfers between devices: 13.3 us -> 0 us
  waiting for transfers between devices: 6.45 us -> 0 us
  blocking collectives: 33.8 us -> 38.6 us
  Pallas kernels: 0 us -> 2.97 us
  matrix products: 1.85 us -> 0 us
  local copies, waits for them, and re-layouts: 3.73 us -> 2.29 us
    all_to_all x2 -> x3, blocking collectives: 18.2 us -> 32.4 us  [exchange(): lax.all_to_all(x, ('row', 'col'), split_axis=0, concat_axis=0, tiled=True)]
    all_to_all x2 -> x0, starting transfers between devices: 13.3 us -> none  [the longest x1 7.28 us: body(): lax.all_to_all(offsets.reshape(share, ncol), 'col', split_axis=1, concat_...]
    all_gather x3 -> x1, blocking collectives: 15.6 us -> 6.2 us  [body(): lax.all_gather(jnp.concatenate([rhs, stiff_diag[None, :]], axis=0), 'row'...]
    all_to_all x2 -> x0, waiting for transfers between devices: 6.45 us -> none  [the longest x1 6.45 us: body(): lax.all_to_all(grouped, 'col', split_axis=2, concat_axis=2, tiled=True)]
    pallas_call x0 -> x4, Pallas kernels: none -> 2.97 us  [the longest x2 1.59 us: body(): pl.pallas_call(functools.partial(middle_kernel, dims, step), out_shape=(m...]
    dot_general x6 -> x0, matrix products: 1.85 us -> none  [the longest x3 1.44 us: body(): jnp.einsum('tij,stj->sti', tile_set, picked, preferred_element_type=jnp.f...]
    gather x3 -> x0, local copies, waits for them, and re-layouts: 1.69 us -> none  [body(): picked = jnp.take(blocks, cols, axis=1)]
    unnamed x10 -> x8, local copies, waits for them, and re-layouts: 1.37 us -> 2.29 us
  transfers between devices with their start and end apart: 2 -> 0, of which waited for: 1 -> 0; matrix products, arithmetic and copies ran while one was open for 3% -> 0% of each run, Pallas kernels for 0% -> 0%
where the time goes in v1:
time: 46.2 us; the launch traced here: 45.9 us
  blocking collectives  38.6 us (84%)
  Pallas kernels  2.97 us (6%)
  local copies, waits for them, and re-layouts  2.29 us (5%)
  between operations  1.29 us (3%)
  other arithmetic  0.7 us (2%)
    all_to_all x3, blocking collectives, exchange(): lax.all_to_all(x, ('row', 'col'), split_axis=0, concat_axis=0, tiled=True)  32.4 us
    all_gather x1, blocking collectives, body(): lax.all_gather(jnp.concatenate([rhs, stiff_diag[None, :]], axis=0), 'row'...  6.2 us
    unnamed x8, local copies, waits for them, and re-layouts  2.29 us
    pallas_call x2, Pallas kernels, body(): pl.pallas_call(functools.partial(middle_kernel, dims, step), out_shape=(m...  1.59 us

profile of v1, /device:TPU:0, one launch (start us, length us, event | category | flops | bytes accessed | tf_op | source)
XLA Modules:
  0.0 45.9 jit_solution(15465988147957310626)
XLA Ops:
  1.3 0.0 copy-start.3
  1.3 0.7 %copy-done.3 = f32[256]{0:T(256)S(1)} copy-done((f32[256]{0:T(256)S(1)}, f32[256]{0:T(256)}, u32[]{:S(2)}) %copy-start.3) | copy-done | bytes 1048
  2.0 0.7 %maximum_bitcast_fusion = f32[1,9,256]{2,1,0:T(8,128)S(1)} fusion(f32[1,256]{1,0:T(1,128)S(1)} %bitcast.17, f32[8,256]{1,0:T(8,128)} %param.6), kind=kLoop, calls=%fused_computation | loop fusion | flops 2304 | bytes 18432
  2.7 6.2 %all-gather.1.packed = f32[4,9,256]{2,1,0:T(8,128)S(1)} all-gather(f32[1,9,256]{2,1,0:T(8,128)S(1)} %maximum_bitcast_fusion), channel_id=2, replica_groups=mesh['row'=4,'col'=8] {'row'}, dimensions={0}, use_global_device_ids=true | all-gather | bytes 46080 | tf_op jit(solution)/shard_map/all_gather | solution.py:148
  8.9 0.0 copy-start.1
  8.9 0.0 copy-start.2
  8.9 0.7 %copy-done.1 = s32[1,1,8]{2,1,0:T(1,128)S(1)} copy-done((s32[1,1,8]{2,1,0:T(1,128)S(1)}, s32[1,1,8]{2,1,0:T(1,128)}, u32[]{:S(2)}) %copy-start.1) | copy-done | bytes 56
  9.5 0.0 copy-done.2
  9.5 0.0 copy-start
  9.5 0.9 %copy-done = bf16[1,1,8,128,128]{4,3,2,1,0:T(8,128)(2,1)S(1)} copy-done((bf16[1,1,8,128,128]{4,3,2,1,0:T(8,128)(2,1)S(1)}, bf16[1,1,8,128,128]{4,3,2,1,0:T(8,128)(2,1)}, u32[]{:S(2)}) %copy-start) | copy-done | bytes 262168
  10.5 0.8 %shard_map.77 = bf16[32,16,128]{2,1,0:T(8,128)(2,1)S(1)} custom-call(s32[8]{0:T(128)S(1)} %bitcast.13, s32[8]{0:T(128)S(1)} %bitcast.16, s32[1]{0:T(128)} %bitcast.7.count, f32[4,9,256]{2,1,0:T(8,128)S(1)} %all-gather.1.packed, bf16[8,128,128]{2,1,0:T(8,128)(2,1)S(1)} %bitcast.10), custom_call_target="tpu_custom_call" | custom-call | tf_op jit(solution)/shard_map/pallas_call | solution.py:149
  11.2 14.0 %all_to_all.15.where.moved = bf16[32,16,128]{2,1,0:T(8,128)(2,1)S(1)} all-to-all(bf16[32,16,128]{2,1,0:T(8,128)(2,1)S(1)} %shard_map.77), channel_id=1, replica_groups=mesh['row'=4,'col'=8] {'row','col'}, dimensions={0} | all-to-all | bytes 262144 | tf_op jit(solution)/shard_map/all_to_all | solution.py:146
  25.2 0.8 %shard_map.78 = (bf16[32,8,128]{2,1,0:T(8,128)(2,1)S(1)}, f32[8,8,128]{2,1,0:T(8,128)S(1)}, f32[8,8,128]{2,1,0:T(8,128)S(1)}, f32[8,8,128]{2,1,0:T(8,128)S(1)}) custom-call(s32[8]{0:T(128)S(1)} %bitcast.14, s32[1]{0:T(128)} %bitcast.8.count, f32[4,9,256]{2,1,0:T(8,128)S(1)} %all-gather.1.packed, bf16[8,128,128]{2,1,0:T(8,128)(2,1)S(1)} %bitcast.11, ...), custom_call_target="tpu_custom_call" | custom-call | tf_op jit(solution)/shard_map/pallas_call | solution.py:161
  26.0 9.5 %all_to_all.16.moved = bf16[32,8,128]{2,1,0:T(8,128)(2,1)S(1)} all-to-all(bf16[32,8,128]{2,1,0:T(8,128)(2,1)S(1)} %get-tuple-element.10), channel_id=1, replica_groups=mesh['row'=4,'col'=8] {'row','col'}, dimensions={0} | all-to-all | bytes 131072 | tf_op jit(solution)/shard_map/all_to_all | solution.py:146
  35.5 0.8 %shard_map.79 = (bf16[32,8,128]{2,1,0:T(8,128)(2,1)S(1)}, f32[8,8,128]{2,1,0:T(8,128)S(1)}, f32[8,8,128]{2,1,0:T(8,128)S(1)}, f32[8,8,128]{2,1,0:T(8,128)S(1)}) custom-call(s32[8]{0:T(128)S(1)} %bitcast.15, s32[1]{0:T(128)} %bitcast.9.count, f32[4,9,256]{2,1,0:T(8,128)S(1)} %all-gather.1.packed, bf16[8,128,128]{2,1,0:T(8,128)(2,1)S(1)} %bitcast.12, ...), custom_call_target="tpu_custom_call" | custom-call | tf_op jit(solution)/shard_map/pallas_call | solution.py:161
  36.3 9.0 %all_to_all.17.moved = bf16[32,8,128]{2,1,0:T(8,128)(2,1)S(1)} all-to-all(bf16[32,8,128]{2,1,0:T(8,128)(2,1)S(1)} %get-tuple-element.14), channel_id=1, replica_groups=mesh['row'=4,'col'=8] {'row','col'}, dimensions={0} | all-to-all | bytes 131072 | tf_op jit(solution)/shard_map/all_to_all | solution.py:146
  45.2 0.6 %shard_map.80 = (f32[8,256]{1,0:T(8,128)}, f32[8,256]{1,0:T(8,128)}) custom-call(f32[4,9,256]{2,1,0:T(8,128)S(1)} %all-gather.1.packed, bf16[32,16,128]{2,1,0:T(8,128)(2,1)S(1)} %all_to_all.15.where.moved, bf16[32,8,128]{2,1,0:T(8,128)(2,1)S(1)} %all_to_all.17.moved, f32[8,8,128]{2,1,0:T(8,128)S(1)} %get-tuple-element.15.old_dir, ...), custom_call_target="tpu_custom_call" | custom-call | tf_op jit(solution)/shard_map/pallas_call | solution.py:171
Async XLA Ops:
  1.3 0.7 %copy-start.3 = (f32[256]{0:T(256)S(1)}, f32[256]{0:T(256)}, u32[]{:S(2)}) copy-start(f32[256]{0:T(256)} %param.7) | copy-start | bytes 3076
  8.9 0.7 %copy-start.1 = (s32[1,1,8]{2,1,0:T(1,128)S(1)}, s32[1,1,8]{2,1,0:T(1,128)}, u32[]{:S(2)}) copy-start(s32[1,1,8]{2,1,0:T(1,128)} %param.9) | copy-start | bytes 100
  8.9 0.7 %copy-start.2 = (s32[1,1,8]{2,1,0:T(1,128)S(1)}, s32[1,1,8]{2,1,0:T(1,128)}, u32[]{:S(2)}) copy-start(s32[1,1,8]{2,1,0:T(1,128)} %param.10) | copy-start | bytes 100
  9.5 0.9 %copy-start = (bf16[1,1,8,128,128]{4,3,2,1,0:T(8,128)(2,1)S(1)}, bf16[1,1,8,128,128]{4,3,2,1,0:T(8,128)(2,1)}, u32[]{:S(2)}) copy-start(bf16[1,1,8,128,128]{4,3,2,1,0:T(8,128)(2,1)} %param.8) | copy-start | bytes 786436

commit v2 on v1

v2 whole, which is shorter than its diff:
```python
import functools

import jax
import jax.numpy as jnp
from jax import lax
from jax.experimental import pallas as pl
from jax.experimental.pallas import tpu as pltpu
from jax.sharding import PartitionSpec as P

STEPS = 3
VMEM_BYTES = 16 << 20

lower_bound = 0.3
upper_bound = 1.9

theta = (upper_bound + lower_bound) / 2.0
delta = (upper_bound - lower_bound) / 2.0
sigma = theta / delta


def coefficients():
    rho = 1.0 / sigma
    out = []
    for _ in range(STEPS - 1):
        rho_new = 1.0 / (2.0 * sigma - rho)
        out.append((rho_new * rho, 2.0 * rho_new / delta))
        rho = rho_new
    return out


def prep_kernel(cols, offsets, count, rhs, diag, tiles, packed, held, column, offset, *scratch):
    line, cols_here, offsets_here, sems = scratch
    samples = rhs.shape[0]
    copies = [
        pltpu.make_async_copy(source, target, sems.at[i])
        for i, (source, target) in enumerate(
            [
                (cols, cols_here),
                (offsets, offsets_here),
                (diag, line),
                (rhs, packed.at[pl.ds(0, samples), :]),
                (tiles.at[0, 0], held),
            ]
        )
    ]
    for copy in copies:
        copy.start()
    for copy in copies[:3]:
        copy.wait()
    packed[samples : samples + 1, :] = line[...]
    for t in range(column.shape[0]):
        here = jnp.where(t < count[0, 0, 0], cols_here[0, 0, t], -1)
        column[t] = jnp.full(column.shape[1:], here, jnp.int32)
        offset[t] = jnp.full(offset.shape[1:], offsets_here[0, 0, t], jnp.int32)
    for copy in copies[3:]:
        copy.wait()


def multiply(directions, tiles, column, out, rows, ncol, offset=None):
    slots = tiles.shape[0]
    samples = column.shape[1]
    for t in range(slots):
        where = column[t]
        picked = jnp.zeros_like(directions[0])
        for j, direction in enumerate(directions):
            picked = jnp.where(where == j, direction, picked)
        sent = lax.dot_general(
            picked.astype(jnp.bfloat16),
            tiles[t],
            (((1,), (1,)), ((), ())),
            preferred_element_type=jnp.float32,
        ).astype(jnp.bfloat16)
        first = (t // ncol) * samples
        for r in range(rows):
            out[r * ncol + t % ncol, pl.ds(first, samples), :] = sent
            if offset is not None:
                half = (slots // ncol) * samples
                out[r * ncol + t % ncol, pl.ds(half + first, samples), :] = (
                    offset[t].astype(jnp.float32).astype(jnp.bfloat16)
                )


def part(packed, r, k, width):
    samples = packed.shape[1] - 1
    rhs = packed[r, :samples, k * width : (k + 1) * width]
    diag = packed[r, samples : samples + 1, k * width : (k + 1) * width]
    return rhs, diag


def coupled(moved, where, r, ncol, share, samples, piece):
    totals = [None] * piece
    for c in range(ncol):
        for a in range(share):
            term = moved[r * ncol + c, pl.ds(a * samples, samples), :].astype(jnp.float32)
            off = where[r * ncol + c, pl.ds((share + a) * samples, samples), :]
            off = off.astype(jnp.float32)
            for k in range(piece):
                mine = jnp.where(off == k, term, 0.0)
                totals[k] = mine if totals[k] is None else totals[k] + mine
    return totals


def first_kernel(dims, packed, tiles, column, offset, out):
    rows, ncol, piece, width = dims
    directions = []
    for r in range(rows):
        for k in range(piece):
            rhs, diag = part(packed, r, k, width)
            directions.append((1.0 / theta) * (1.0 / diag) * rhs)
    multiply(directions, tiles, column, out, rows, ncol, offset)


def middle_kernel(dims, step, packed, tiles, column, where, moved, *refs):
    rows, ncol, piece, width = dims
    samples = packed.shape[1] - 1
    share = tiles.shape[0] // ncol
    a, b = coefficients()[step]
    if step == 0:
        out, new_dir, new_res, new_sol = refs
    else:
        old_dir, old_res, old_sol, out, new_dir, new_res, new_sol = refs
    directions = []
    for r in range(rows):
        image = coupled(moved, where, r, ncol, share, samples, piece)
        for k in range(piece):
            rhs, diag = part(packed, r, k, width)
            inverse = 1.0 / diag
            i = r * piece + k
            if step == 0:
                direction = (1.0 / theta) * inverse * rhs
                residual = rhs
                total = direction
            else:
                direction, residual, total = old_dir[i], old_res[i], old_sol[i]
            residual = residual - (diag * direction + image[k])
            direction = a * direction + b * inverse * residual
            new_dir[i] = direction
            new_res[i] = residual
            new_sol[i] = total + direction
            directions.append(direction)
    multiply(directions, tiles, column, out, rows, ncol)


def last_kernel(dims, share, packed, where, moved, old_dir, old_res, old_sol, solution, residual):
    rows, ncol, piece, width = dims
    samples = packed.shape[1] - 1
    me = lax.axis_index("row")
    image = coupled(moved, where, me, ncol, share, samples, piece)
    for k in range(piece):
        lanes = slice(k * width, (k + 1) * width)
        diag = packed[me, samples : samples + 1, lanes]
        i = me * piece + k
        solution[:, lanes] = old_sol[i]
        residual[:, lanes] = old_res[i] - (diag * old_dir[i] + image[k])


def body(rhs, stiff_diag, tiles, tile_cols, tile_offsets, tile_counts):
    slots, width = tiles.shape[2:4]
    rows, ncol = lax.axis_size("row"), lax.axis_size("col")
    share = slots // ncol
    piece = stiff_diag.shape[0] // width
    samples = rhs.shape[0]
    blocks = rows * piece
    dims = (rows, ncol, piece, width)
    vmem = pl.BlockSpec(memory_space=pltpu.VMEM)
    hbm = pl.BlockSpec(memory_space=pltpu.HBM)
    state = jax.ShapeDtypeStruct((blocks, samples, width), jnp.float32)
    table = jax.ShapeDtypeStruct((slots, samples, width), jnp.int32)
    message = jax.ShapeDtypeStruct((rows * ncol, share * samples, width), jnp.bfloat16)
    wide = jax.ShapeDtypeStruct((rows * ncol, 2 * share * samples, width), jnp.bfloat16)
    params = pltpu.CompilerParams(vmem_limit_bytes=VMEM_BYTES)

    def exchange(x):
        return lax.all_to_all(x, ("row", "col"), split_axis=0, concat_axis=0, tiled=True)

    def far(x):
        return pltpu.with_memory_space_constraint(x, pltpu.HBM)

    packed, held, column, offset = pl.pallas_call(
        prep_kernel,
        out_shape=(
            jax.ShapeDtypeStruct((samples + 1, rhs.shape[1]), jnp.float32),
            jax.ShapeDtypeStruct(tiles.shape[2:], tiles.dtype),
            table,
            table,
        ),
        in_specs=[hbm] * 2 + [pl.BlockSpec(memory_space=pltpu.SMEM)] + [hbm] * 3,
        out_specs=(vmem,) * 4,
        scratch_shapes=[
            pltpu.VMEM((1, rhs.shape[1]), jnp.float32),
            pltpu.SMEM(tile_cols.shape, jnp.int32),
            pltpu.SMEM(tile_offsets.shape, jnp.int32),
            pltpu.SemaphoreType.DMA((5,)),
        ],
        compiler_params=params,
    )(far(tile_cols), far(tile_offsets), tile_counts, far(rhs), far(stiff_diag[None, :]), far(tiles))
    packed = lax.all_gather(packed, "row", axis=0)
    sent = pl.pallas_call(
        functools.partial(first_kernel, dims),
        out_shape=wide,
        in_specs=[vmem] * 4,
        out_specs=vmem,
        compiler_params=params,
    )(packed, held, column, offset)
    moved = where = exchange(sent)
    states = ()
    for step in range(STEPS - 1):
        sent, *states = pl.pallas_call(
            functools.partial(middle_kernel, dims, step),
            out_shape=(message, state, state, state),
            in_specs=[vmem] * (5 + len(states)),
            out_specs=(vmem,) * 4,
            compiler_params=params,
        )(packed, held, column, where, moved, *states)
        moved = exchange(sent)
    out = jax.ShapeDtypeStruct(rhs.shape, jnp.float32)
    return pl.pallas_call(
        functools.partial(last_kernel, dims, share),
        out_shape=(out, out),
        in_specs=[vmem] * (3 + len(states)),
        out_specs=(vmem, vmem),
        compiler_params=params,
    )(packed, where, moved, *states)


def solution(mesh):
    in_specs = (
        P(None, ("row", "col")),
        P(("row", "col")),
        P("row", "col", None, None, None),
        P("row", "col", None),
        P("row", "col", None),
        P("row", "col", None),
    )
    out_specs = (P(None, ("row", "col")), P(None, ("row", "col")))
    return jax.shard_map(body, mesh=mesh, in_specs=in_specs, out_specs=out_specs, check_vma=False)
```

time: 46.2 us -> 42.5 us (0.920)
  local copies, waits for them, and re-layouts: 2.29 us -> 0 us
  other arithmetic: 0.7 us -> 0 us
  Pallas kernels: 2.97 us -> 2.36 us
    unnamed x8 -> x0, local copies, waits for them, and re-layouts: 2.29 us -> none
    pallas_call x2, Pallas kernels: 1.59 us -> 0.48 us  [body(): pl.pallas_call(functools.partial(middle_kernel, dims, step), out_shape=(m...]
    pallas_call x0 -> x1, Pallas kernels: none -> 1.03 us  [body(): pl.pallas_call(prep_kernel, out_shape=(jax.ShapeDtypeStruct((samples + 1,...]
    unnamed x1 -> x0, other arithmetic: 0.7 us -> none
    pallas_call x1, Pallas kernels: 0.77 us -> 0.23 us  [body(): pl.pallas_call(functools.partial(first_kernel, dims), out_shape=wide, in_...]
where the time goes in v2:
time: 42.5 us; the launch traced here: 42.3 us
  blocking collectives  38.6 us (91%)
  Pallas kernels  2.36 us (6%)
  between operations  1.29 us (3%)
    all_to_all x3, blocking collectives, exchange(): lax.all_to_all(x, ('row', 'col'), split_axis=0, concat_axis=0, tiled=True)  32.4 us
    all_gather x1, blocking collectives, body(): packed = lax.all_gather(packed, 'row', axis=0)  6.22 us
    pallas_call x1, Pallas kernels, body(): pl.pallas_call(prep_kernel, out_shape=(jax.ShapeDtypeStruct((samples + 1,...  1.03 us

profile of v2, /device:TPU:0, one launch (start us, length us, event | category | flops | bytes accessed | tf_op | source)
XLA Modules:
  0.0 42.3 jit_solution(17471113965414012744)
XLA Ops:
  1.3 1.0 %shard_map.77 = (f32[9,256]{1,0:T(8,128)S(1)}, bf16[8,128,128]{2,1,0:T(8,128)(2,1)S(1)}, s32[8,8,128]{2,1,0:T(8,128)S(1)}, s32[8,8,128]{2,1,0:T(8,128)S(1)}) custom-call(s32[1,1,8]{2,1,0:T(1,128)} %cols.1, s32[1,1,8]{2,1,0:T(1,128)} %offsets.1, s32[1,1,1]{2,1,0:T(1,128)S(6)} %copy.8.count, f32[8,256]{1,0:T(8,128)} %rhs.1, f32[1,256]{1,0:T(1,128)} %bitcast.3, ...), custom_call_target="tpu_custom_call" | custom-call | tf_op jit(solution)/shard_map/pallas_call | solution.py:179
  2.3 6.2 %all-gather.1.packed = f32[4,9,256]{2,1,0:T(8,128)S(1)} all-gather(f32[1,9,256]{2,1,0:T(8,128)S(1)} %bitcast.2), channel_id=2, replica_groups=mesh['row'=4,'col'=8] {'row'}, dimensions={0}, use_global_device_ids=true | all-gather | bytes 46080 | tf_op jit(solution)/shard_map/all_gather | solution.py:197
  8.5 0.2 shard_map.78
  8.8 14.0 %all_to_all.15.where.moved = bf16[32,16,128]{2,1,0:T(8,128)(2,1)S(1)} all-to-all(bf16[32,16,128]{2,1,0:T(8,128)(2,1)S(1)} %shard_map.78), channel_id=1, replica_groups=mesh['row'=4,'col'=8] {'row','col'}, dimensions={0} | all-to-all | bytes 262144 | tf_op jit(solution)/shard_map/all_to_all | solution.py:174
  22.7 0.2 shard_map.79
  23.0 9.5 %all_to_all.16.moved = bf16[32,8,128]{2,1,0:T(8,128)(2,1)S(1)} all-to-all(bf16[32,8,128]{2,1,0:T(8,128)(2,1)S(1)} %get-tuple-element.18), channel_id=1, replica_groups=mesh['row'=4,'col'=8] {'row','col'}, dimensions={0} | all-to-all | bytes 131072 | tf_op jit(solution)/shard_map/all_to_all | solution.py:174
  32.4 0.2 shard_map.80
  32.7 9.0 %all_to_all.17.moved = bf16[32,8,128]{2,1,0:T(8,128)(2,1)S(1)} all-to-all(bf16[32,8,128]{2,1,0:T(8,128)(2,1)S(1)} %get-tuple-element.22), channel_id=1, replica_groups=mesh['row'=4,'col'=8] {'row','col'}, dimensions={0} | all-to-all | bytes 131072 | tf_op jit(solution)/shard_map/all_to_all | solution.py:174
  41.7 0.6 %shard_map.81 = (f32[8,256]{1,0:T(8,128)}, f32[8,256]{1,0:T(8,128)}) custom-call(f32[4,9,256]{2,1,0:T(8,128)S(1)} %all-gather.1.packed, bf16[32,16,128]{2,1,0:T(8,128)(2,1)S(1)} %all_to_all.15.where.moved, bf16[32,8,128]{2,1,0:T(8,128)(2,1)S(1)} %all_to_all.17.moved, f32[8,8,128]{2,1,0:T(8,128)S(1)} %get-tuple-element.23.old_dir, ...), custom_call_target="tpu_custom_call" | custom-call | tf_op jit(solution)/shard_map/pallas_call | solution.py:217

commit v3 on v2

v3 whole, which is shorter than its diff:
```python
import functools

import jax
import jax.numpy as jnp
from jax import lax
from jax.experimental import pallas as pl
from jax.experimental.pallas import tpu as pltpu
from jax.sharding import PartitionSpec as P

STEPS = 3
VMEM_BYTES = 16 << 20
PAIR = 2

lower_bound = 0.3
upper_bound = 1.9

theta = (upper_bound + lower_bound) / 2.0
delta = (upper_bound - lower_bound) / 2.0
sigma = theta / delta


def coefficients():
    rho = 1.0 / sigma
    out = []
    for _ in range(STEPS - 1):
        rho_new = 1.0 / (2.0 * sigma - rho)
        out.append((rho_new * rho, 2.0 * rho_new / delta))
        rho = rho_new
    return out


def pack_kernel(rhs, diag, packed, line, sems):
    samples = rhs.shape[0]
    copies = [
        pltpu.make_async_copy(diag, line, sems.at[0]),
        pltpu.make_async_copy(rhs, packed.at[pl.ds(0, samples), :], sems.at[1]),
    ]
    for copy in copies:
        copy.start()
    copies[0].wait()
    packed[samples : samples + 1, :] = line[...]
    copies[1].wait()


def prep_kernel(piece, cols, offsets, count, tiles, held, column, offset, *scratch):
    cols_here, offsets_here, sems = scratch
    me = lax.axis_index("row")
    copies = [
        pltpu.make_async_copy(source, target, sems.at[i])
        for i, (source, target) in enumerate(
            [(cols, cols_here), (offsets, offsets_here), (tiles.at[0, 0], held)]
        )
    ]
    for copy in copies:
        copy.start()
    for copy in copies[:2]:
        copy.wait()
    for t in range(column.shape[0]):
        col = cols_here[0, 0, t]
        col = ((col // piece) ^ me) * piece + col % piece
        here = jnp.where(t < count[0, 0, 0], col, -1)
        column[t] = jnp.full(column.shape[1:], here, jnp.int32)
        offset[t] = jnp.full(offset.shape[1:], offsets_here[0, 0, t], jnp.int32)
    copies[2].wait()


def multiply(directions, tiles, column, out, rows, ncol, offset=None):
    slots = tiles.shape[0]
    samples = column.shape[1]
    for t in range(slots):
        where = column[t]
        picked = jnp.zeros_like(directions[0])
        for j, direction in enumerate(directions):
            picked = jnp.where(where == j, direction, picked)
        sent = lax.dot_general(
            picked.astype(jnp.bfloat16),
            tiles[t],
            (((1,), (1,)), ((), ())),
            preferred_element_type=jnp.float32,
        ).astype(jnp.bfloat16)
        first = (t // ncol) * samples
        for r in range(rows):
            place = r * ncol + t % ncol
            if offset is None:
                out[place, pl.ds(first, samples), :] = sent
            else:
                pairs = samples // PAIR
                first = (t // ncol) * (pairs + 1)
                out[place, pl.ds(first, pairs)] = sent.reshape(pairs, PAIR, sent.shape[1])
                out[place, first + pairs] = offset[t][:PAIR].astype(jnp.float32).astype(jnp.bfloat16)


def part(packed, k, width):
    samples = packed.shape[0] - 1
    rhs = packed[:samples, k * width : (k + 1) * width]
    diag = packed[samples : samples + 1, k * width : (k + 1) * width]
    return rhs, diag


def coupled(moved, where, r, ncol, share, samples, piece):
    totals = [None] * piece
    pairs = samples // PAIR
    for c in range(ncol):
        for a in range(share):
            place = r * ncol + c
            first = a * (pairs + 1)
            off = where[place, first + pairs].astype(jnp.float32)[:1]
            if moved is where:
                term = moved[place, pl.ds(first, pairs)].reshape(samples, off.shape[1])
            else:
                term = moved[place, pl.ds(a * samples, samples), :]
            term = term.astype(jnp.float32)
            for k in range(piece):
                mine = jnp.where(off == k, term, 0.0)
                totals[k] = mine if totals[k] is None else totals[k] + mine
    return totals


def first_kernel(dims, *refs):
    rows, ncol, piece, width = dims
    packed = refs[:rows]
    tiles, column, offset, out = refs[rows:]
    directions = []
    for p in range(rows):
        for k in range(piece):
            rhs, diag = part(packed[p], k, width)
            directions.append((1.0 / theta) * (1.0 / diag) * rhs)
    multiply(directions, tiles, column, out, rows, ncol, offset)


def middle_kernel(dims, step, *refs):
    rows, ncol, piece, width = dims
    packed = refs[:rows]
    tiles, column, where, moved = refs[rows : rows + 4]
    if step == 0:
        moved = where
    samples = packed[0].shape[0] - 1
    share = tiles.shape[0] // ncol
    a, b = coefficients()[step]
    if step == 0:
        out, new_dir, new_res, new_sol = refs[rows + 4 :]
    else:
        old_dir, old_res, old_sol, out, new_dir, new_res, new_sol = refs[rows + 4 :]
    me = lax.axis_index("row")
    directions = []
    for p in range(rows):
        image = coupled(moved, where, me ^ p, ncol, share, samples, piece)
        for k in range(piece):
            rhs, diag = part(packed[p], k, width)
            inverse = 1.0 / diag
            i = p * piece + k
            if step == 0:
                direction = (1.0 / theta) * inverse * rhs
                residual = rhs
                total = direction
            else:
                direction, residual, total = old_dir[i], old_res[i], old_sol[i]
            residual = residual - (diag * direction + image[k])
            direction = a * direction + b * inverse * residual
            new_dir[i] = direction
            new_res[i] = residual
            new_sol[i] = total + direction
            directions.append(direction)
    multiply(directions, tiles, column, out, rows, ncol)


def last_kernel(dims, share, packed, where, moved, old_dir, old_res, old_sol, solution, residual):
    rows, ncol, piece, width = dims
    samples = packed.shape[0] - 1
    me = lax.axis_index("row")
    image = coupled(moved, where, me, ncol, share, samples, piece)
    for k in range(piece):
        lanes = slice(k * width, (k + 1) * width)
        diag = packed[samples : samples + 1, lanes]
        solution[:, lanes] = old_sol[k]
        residual[:, lanes] = old_res[k] - (diag * old_dir[k] + image[k])


def body(rhs, stiff_diag, tiles, tile_cols, tile_offsets, tile_counts):
    slots, width = tiles.shape[2:4]
    rows, ncol = lax.axis_size("row"), lax.axis_size("col")
    share = slots // ncol
    piece = stiff_diag.shape[0] // width
    samples = rhs.shape[0]
    blocks = rows * piece
    dims = (rows, ncol, piece, width)
    vmem = pl.BlockSpec(memory_space=pltpu.VMEM)
    hbm = pl.BlockSpec(memory_space=pltpu.HBM)
    state = jax.ShapeDtypeStruct((blocks, samples, width), jnp.float32)
    table = jax.ShapeDtypeStruct((slots, samples, width), jnp.int32)
    message = jax.ShapeDtypeStruct((rows * ncol, share * samples, width), jnp.bfloat16)
    wide = jax.ShapeDtypeStruct(
        (rows * ncol, share * (samples // PAIR + 1), PAIR, width), jnp.bfloat16
    )
    params = pltpu.CompilerParams(vmem_limit_bytes=VMEM_BYTES)

    def exchange(x):
        return lax.all_to_all(x, ("row", "col"), split_axis=0, concat_axis=0, tiled=True)

    def far(x):
        return pltpu.with_memory_space_constraint(x, pltpu.HBM)

    packed = pl.pallas_call(
        pack_kernel,
        out_shape=jax.ShapeDtypeStruct((samples + 1, rhs.shape[1]), jnp.float32),
        in_specs=[hbm] * 2,
        out_specs=vmem,
        scratch_shapes=[
            pltpu.VMEM((1, rhs.shape[1]), jnp.float32),
            pltpu.SemaphoreType.DMA((2,)),
        ],
        compiler_params=params,
    )(far(rhs), far(stiff_diag[None, :]))
    held, column, offset = pl.pallas_call(
        functools.partial(prep_kernel, piece),
        out_shape=(jax.ShapeDtypeStruct(tiles.shape[2:], tiles.dtype), table, table),
        in_specs=[hbm] * 2 + [pl.BlockSpec(memory_space=pltpu.SMEM)] + [hbm],
        out_specs=(vmem,) * 3,
        scratch_shapes=[
            pltpu.SMEM(tile_cols.shape, jnp.int32),
            pltpu.SMEM(tile_offsets.shape, jnp.int32),
            pltpu.SemaphoreType.DMA((3,)),
        ],
        compiler_params=params,
        cost_estimate=pl.CostEstimate(flops=0, bytes_accessed=4 << 20, transcendentals=0),
    )(far(tile_cols), far(tile_offsets), tile_counts, far(tiles))

    pieces = {0: packed}
    bit = rows // 2
    while bit:
        swap = [(i, i ^ bit) for i in range(rows)]
        for p in sorted(pieces):
            pieces[p ^ bit] = lax.ppermute(pieces[p], "row", swap)
        if bit == rows // 2:
            pieces[bit], held, column, offset = lax.optimization_barrier(
                (pieces[bit], held, column, offset)
            )
        bit //= 2
    pieces = [pieces[p] for p in range(rows)]
    sent = pl.pallas_call(
        functools.partial(first_kernel, dims),
        out_shape=wide,
        in_specs=[vmem] * (rows + 3),
        out_specs=vmem,
        compiler_params=params,
    )(*pieces, held, column, offset)
    moved = where = exchange(sent)
    states = ()
    for step in range(STEPS - 1):
        sent, *states = pl.pallas_call(
            functools.partial(middle_kernel, dims, step),
            out_shape=(message, state, state, state),
            in_specs=[vmem] * (rows + 4 + len(states)),
            out_specs=(vmem,) * 4,
            compiler_params=params,
        )(*pieces, held, column, where, moved, *states)
        moved = exchange(sent)
    out = jax.ShapeDtypeStruct(rhs.shape, jnp.float32)
    return pl.pallas_call(
        functools.partial(last_kernel, dims, share),
        out_shape=(out, out),
        in_specs=[vmem] * (3 + len(states)),
        out_specs=(vmem, vmem),
        compiler_params=params,
    )(packed, where, moved, *states)


def solution(mesh):
    in_specs = (
        P(None, ("row", "col")),
        P(("row", "col")),
        P("row", "col", None, None, None),
        P("row", "col", None),
        P("row", "col", None),
        P("row", "col", None),
    )
    out_specs = (P(None, ("row", "col")), P(None, ("row", "col")))
    return jax.shard_map(body, mesh=mesh, in_specs=in_specs, out_specs=out_specs, check_vma=False)
```

time: 42.5 us -> 40.6 us (0.955)
  blocking collectives: 38.6 us -> 31.4 us
  starting transfers between devices: 0 us -> 3.57 us
  waiting for transfers between devices: 0 us -> 0.91 us
  Pallas kernels: 2.36 us -> 3.18 us
    all_gather x1 -> x0, blocking collectives: 6.22 us -> none  [body(): packed = lax.all_gather(packed, 'row', axis=0)]
    ppermute x0 -> x3, starting transfers between devices: none -> 3.57 us  [body(): pieces[p ^ bit] = lax.ppermute(pieces[p], 'row', swap)]
    all_to_all x3, blocking collectives: 32.4 us -> 31.4 us  [exchange(): lax.all_to_all(x, ('row', 'col'), split_axis=0, concat_axis=0, tiled=True)]
    ppermute x0 -> x3, waiting for transfers between devices: none -> 0.91 us  [body(): pieces[p ^ bit] = lax.ppermute(pieces[p], 'row', swap)]
    pallas_call x1 -> x2, Pallas kernels: 1.03 us -> 1.71 us  [the longest x1 0.98 us: body(): pl.pallas_call(functools.partial(prep_kernel, piece), out_shape=(jax.Shap...]
  transfers between devices with their start and end apart: 0 -> 3, of which waited for: 0 -> 2; matrix products, arithmetic and copies ran while one was open for 0% -> 0% of each run, Pallas kernels for 0% -> 2%
where the time goes in v3:
time: 40.6 us; the launch traced here: 40.3 us
  blocking collectives  31.4 us (77%)
  starting transfers between devices  3.57 us (9%)
  Pallas kernels  3.18 us (8%)
  between operations  1.31 us (3%)
  waiting for transfers between devices  0.91 us (2%)
    all_to_all x3, blocking collectives, exchange(): lax.all_to_all(x, ('row', 'col'), split_axis=0, concat_axis=0, tiled=True)  31.4 us
    ppermute x3, starting transfers between devices, body(): pieces[p ^ bit] = lax.ppermute(pieces[p], 'row', swap)  3.57 us
    pallas_call x1, Pallas kernels, body(): pl.pallas_call(functools.partial(prep_kernel, piece), out_shape=(jax.Shap...  0.98 us
    ppermute x3, waiting for transfers between devices, body(): pieces[p ^ bit] = lax.ppermute(pieces[p], 'row', swap)  0.91 us
  transfers between devices with their start and end apart: 3, of which 2 were waited for; matrix products, arithmetic and copies ran while one was open for 0% of the time, Pallas kernels for 2%

profile of v3, /device:TPU:0, one launch (start us, length us, event | category | flops | bytes accessed | tf_op | source)
XLA Modules:
  0.0 40.3 jit_solution(16352198912012788470)
XLA Ops:
  0.6 0.7 %shard_map.77.refs_0_.packed = f32[9,256]{1,0:T(8,128)S(1)} custom-call(f32[8,256]{1,0:T(8,128)} %rhs.1, f32[1,256]{1,0:T(1,128)} %bitcast.1), custom_call_target="tpu_custom_call" | custom-call | tf_op jit(solution)/shard_map/pallas_call | solution.py:203
  1.4 3.1 %collective-permute-start.1 = (f32[9,256]{1,0:T(8,128)S(1)}, f32[9,256]{1,0:T(8,128)S(1)}, u32[]{:S(2)}, u32[]{:S(2)}) collective-permute-start(f32[9,256]{1,0:T(8,128)S(1)} %shard_map.77.refs_0_.packed), channel_id=1, source_target_pairs={{0,16},{8,24},{16,0},{24,8},{1,17},{9,25},{17,1},{25,9},{2,18},{10... | collective-permute-start | bytes 27656 | tf_op jit(solution)/shard_map/ppermute | solution.py:233
  4.4 0.0 collective-permute-start
  5.1 1.0 %shard_map.78 = (bf16[8,128,128]{2,1,0:T(8,128)(2,1)S(1)}, s32[8,8,128]{2,1,0:T(8,128)S(1)}, s32[8,8,128]{2,1,0:T(8,128)S(1)}) custom-call(s32[1,1,8]{2,1,0:T(1,128)} %cols.1, s32[1,1,8]{2,1,0:T(1,128)} %offsets.1, s32[1,1,1]{2,1,0:T(1,128)S(6)} %copy.8.count, bf16[1,1,8,128,128]{4,3,2,1,0:T(8,128)(2,1)} %tiles.1), custom_call_target="tpu_custom_call" | custom-call | bytes 4194304 | tf_op jit(solution)/shard_map/pallas_call | solution.py:214
  6.1 0.1 collective-permute-done.1.refs_2_
  6.1 0.5 %collective-permute-start.2 = (f32[9,256]{1,0:T(8,128)S(1)}, f32[9,256]{1,0:T(8,128)S(1)}, u32[]{:S(2)}, u32[]{:S(2)}) collective-permute-start(f32[9,256]{1,0:T(8,128)S(1)} %collective-permute-done.1.refs_2_), channel_id=1, source_target_pairs={{0,8},{8,0},{16,24},{24,16},{1,9},{9,1},{17,25},{25,17},{2,10},{10... | collective-permute-start | bytes 27656 | tf_op jit(solution)/shard_map/ppermute | solution.py:233
  6.7 0.0 collective-permute-done.refs_1_
  6.7 0.8 %collective-permute-done.2.refs_3_ = f32[9,256]{1,0:T(8,128)S(1)} collective-permute-done((f32[9,256]{1,0:T(8,128)S(1)}, f32[9,256]{1,0:T(8,128)S(1)}, u32[]{:S(2)}, u32[]{:S(2)}) %collective-permute-start.2) | collective-permute-done | bytes 9248 | tf_op jit(solution)/shard_map/ppermute | solution.py:233
  7.5 0.3 shard_map.79
  7.8 13.4 %all_to_all.15.refs_6_.refs_7_.where = bf16[32,5,2,128]{3,2,1,0:T(2,128)(2,1)S(1)} all-to-all(bf16[32,5,2,128]{3,2,1,0:T(2,128)(2,1)S(1)} %shard_map.79), channel_id=1, replica_groups=mesh['row'=4,'col'=8] {'row','col'}, dimensions={0} | all-to-all | bytes 163840 | tf_op jit(solution)/shard_map/all_to_all | solution.py:198
  21.2 0.3 shard_map.80
  21.5 9.0 %all_to_all.16.refs_7_ = bf16[32,8,128]{2,1,0:T(8,128)(2,1)S(1)} all-to-all(bf16[32,8,128]{2,1,0:T(8,128)(2,1)S(1)} %get-tuple-element.24), channel_id=1, replica_groups=mesh['row'=4,'col'=8] {'row','col'}, dimensions={0} | all-to-all | bytes 131072 | tf_op jit(solution)/shard_map/all_to_all | solution.py:198
  30.5 0.3 shard_map.81
  30.7 9.0 %all_to_all.17.moved = bf16[32,8,128]{2,1,0:T(8,128)(2,1)S(1)} all-to-all(bf16[32,8,128]{2,1,0:T(8,128)(2,1)S(1)} %get-tuple-element.28), channel_id=1, replica_groups=mesh['row'=4,'col'=8] {'row','col'}, dimensions={0} | all-to-all | bytes 131072 | tf_op jit(solution)/shard_map/all_to_all | solution.py:198
  39.7 0.6 %shard_map.82 = (f32[8,256]{1,0:T(8,128)}, f32[8,256]{1,0:T(8,128)}) custom-call(f32[9,256]{1,0:T(8,128)S(1)} %shard_map.77.refs_0_.packed, bf16[32,5,2,128]{3,2,1,0:T(2,128)(2,1)S(1)} %all_to_all.15.refs_6_.refs_7_.where, bf16[32,8,128]{2,1,0:T(8,128)(2,1)S(1)} %all_to_all.17.moved, f32[8,8,128]{2,1,0:T(8,128)S(1)} %get-tuple-element.29.old_dir, ...), custom_call_target="tpu_custom_call" | custom-call | tf_op jit(solution)/shard_map/pallas_call | solution.py:259
Async XLA Ops:
  1.4 4.8 %collective-permute-start.1 = (f32[9,256]{1,0:T(8,128)S(1)}, f32[9,256]{1,0:T(8,128)S(1)}, u32[]{:S(2)}, u32[]{:S(2)}) collective-permute-start(f32[9,256]{1,0:T(8,128)S(1)} %shard_map.77.refs_0_.packed), channel_id=1, source_target_pairs={{0,16},{8,24},{16,0},{24,8},{1,17},{9,25},{17,1},{25,9},{2,18},{10... | collective-permute-start | bytes 27656 | tf_op jit(solution)/shard_map/ppermute | solution.py:233
  4.4 2.2 %collective-permute-start = (f32[9,256]{1,0:T(8,128)S(1)}, f32[9,256]{1,0:T(8,128)S(1)}, u32[]{:S(2)}, u32[]{:S(2)}) collective-permute-start(f32[9,256]{1,0:T(8,128)S(1)} %shard_map.77.refs_0_.packed), channel_id=1, source_target_pairs={{0,8},{8,0},{16,24},{24,16},{1,9},{9,1},{17,25},{25,17},{2,10},{10... | collective-permute-start | bytes 27656 | tf_op jit(solution)/shard_map/ppermute | solution.py:233
  6.1 1.3 %collective-permute-start.2 = (f32[9,256]{1,0:T(8,128)S(1)}, f32[9,256]{1,0:T(8,128)S(1)}, u32[]{:S(2)}, u32[]{:S(2)}) collective-permute-start(f32[9,256]{1,0:T(8,128)S(1)} %collective-permute-done.1.refs_2_), channel_id=1, source_target_pairs={{0,8},{8,0},{16,24},{24,16},{1,9},{9,1},{17,25},{25,17},{2,10},{10... | collective-permute-start | bytes 27656 | tf_op jit(solution)/shard_map/ppermute | solution.py:233

commit v4 on v3

--- a/solution.py
+++ b/solution.py
@@ -97,7 +97,7 @@
     return rhs, diag
 
 
-def coupled(moved, where, r, ncol, share, samples, piece):
+def coupled(moved, where, r, ncol, share, samples, piece, base=None):
     totals = [None] * piece
     pairs = samples // PAIR
     for c in range(ncol):
@@ -108,7 +108,8 @@
             if moved is where:
                 term = moved[place, pl.ds(first, pairs)].reshape(samples, off.shape[1])
             else:
-                term = moved[place, pl.ds(a * samples, samples), :]
+                here = place if base is None else base + c
+                term = moved[here, pl.ds(a * samples, samples), :]
             term = term.astype(jnp.float32)
             for k in range(piece):
                 mine = jnp.where(off == k, term, 0.0)
@@ -161,14 +162,14 @@
             new_res[i] = residual
             new_sol[i] = total + direction
             directions.append(direction)
-    multiply(directions, tiles, column, out, rows, ncol)
+    multiply(directions, tiles, column, out, out.shape[0] // ncol, ncol)
 
 
 def last_kernel(dims, share, packed, where, moved, old_dir, old_res, old_sol, solution, residual):
     rows, ncol, piece, width = dims
     samples = packed.shape[0] - 1
     me = lax.axis_index("row")
-    image = coupled(moved, where, me, ncol, share, samples, piece)
+    image = coupled(moved, where, me, ncol, share, samples, piece, 0)
     for k in range(piece):
         lanes = slice(k * width, (k + 1) * width)
         diag = packed[samples : samples + 1, lanes]
@@ -188,14 +189,15 @@
     hbm = pl.BlockSpec(memory_space=pltpu.HBM)
     state = jax.ShapeDtypeStruct((blocks, samples, width), jnp.float32)
     table = jax.ShapeDtypeStruct((slots, samples, width), jnp.int32)
+    narrow = jax.ShapeDtypeStruct((ncol, share * samples, width), jnp.bfloat16)
     message = jax.ShapeDtypeStruct((rows * ncol, share * samples, width), jnp.bfloat16)
     wide = jax.ShapeDtypeStruct(
         (rows * ncol, share * (samples // PAIR + 1), PAIR, width), jnp.bfloat16
     )
     params = pltpu.CompilerParams(vmem_limit_bytes=VMEM_BYTES)
 
-    def exchange(x):
-        return lax.all_to_all(x, ("row", "col"), split_axis=0, concat_axis=0, tiled=True)
+    def exchange(x, axes=("row", "col")):
+        return lax.all_to_all(x, axes, split_axis=0, concat_axis=0, tiled=True)
 
     def far(x):
         return pltpu.with_memory_space_constraint(x, pltpu.HBM)
@@ -226,16 +228,8 @@
     )(far(tile_cols), far(tile_offsets), tile_counts, far(tiles))
 
     pieces = {0: packed}
-    bit = rows // 2
-    while bit:
-        swap = [(i, i ^ bit) for i in range(rows)]
-        for p in sorted(pieces):
-            pieces[p ^ bit] = lax.ppermute(pieces[p], "row", swap)
-        if bit == rows // 2:
-            pieces[bit], held, column, offset = lax.optimization_barrier(
-                (pieces[bit], held, column, offset)
-            )
-        bit //= 2
+    for p in range(1, rows):
+        pieces[p] = lax.ppermute(packed, "row", [(i, i ^ p) for i in range(rows)])
     pieces = [pieces[p] for p in range(rows)]
     sent = pl.pallas_call(
         functools.partial(first_kernel, dims),
@@ -249,12 +243,12 @@
     for step in range(STEPS - 1):
         sent, *states = pl.pallas_call(
             functools.partial(middle_kernel, dims, step),
-            out_shape=(message, state, state, state),
+            out_shape=(message if step + 2 < STEPS else narrow, state, state, state),
             in_specs=[vmem] * (rows + 4 + len(states)),
             out_specs=(vmem,) * 4,
             compiler_params=params,
         )(*pieces, held, column, where, moved, *states)
-        moved = exchange(sent)
+        moved = exchange(sent, ("row", "col") if step + 2 < STEPS else "col")
     out = jax.ShapeDtypeStruct(rhs.shape, jnp.float32)
     return pl.pallas_call(
         functools.partial(last_kernel, dims, share),

time: 40.6 us -> 39.5 us (0.973)
  blocking collectives: 31.4 us -> 30.1 us
  waiting for transfers between devices: 0.91 us -> 1.41 us
    all_to_all x3, blocking collectives: 31.4 us -> 30.1 us  [exchange(): return lax.all_to_all(x, axes, split_axis=0, concat_axis=0, tiled=True)]
    ppermute x3, waiting for transfers between devices: 0.91 us -> 1.41 us  [body(): pieces[p] = lax.ppermute(packed, 'row', [(i, i ^ p) for i in range(rows)])]
  transfers between devices with their start and end apart: 3 -> 3, of which waited for: 2 -> 1; matrix products, arithmetic and copies ran while one was open for 0% -> 0% of each run, Pallas kernels for 2% -> 3%
where the time goes in v4:
time: 39.5 us; the launch traced here: 39.2 us
  blocking collectives  30.1 us (76%)
  Pallas kernels  3.18 us (8%)
  starting transfers between devices  3.18 us (8%)
  waiting for transfers between devices  1.41 us (4%)
  between operations  1.32 us (3%)
    all_to_all x3, blocking collectives, exchange(): return lax.all_to_all(x, axes, split_axis=0, concat_axis=0, tiled=True)  30.1 us
    ppermute x3, starting transfers between devices, body(): pieces[p] = lax.ppermute(packed, 'row', [(i, i ^ p) for i in range(rows)])  3.18 us
    ppermute x3, waiting for transfers between devices, body(): pieces[p] = lax.ppermute(packed, 'row', [(i, i ^ p) for i in range(rows)])  1.41 us
    pallas_call x1, Pallas kernels, body(): pl.pallas_call(functools.partial(prep_kernel, piece), out_shape=(jax.Shap...  0.98 us
  transfers between devices with their start and end apart: 3, of which 1 were waited for; matrix products, arithmetic and copies ran while one was open for 0% of the time, Pallas kernels for 3%

profile of v4, /device:TPU:0, one launch (start us, length us, event | category | flops | bytes accessed | tf_op | source)
XLA Modules:
  0.0 39.2 jit_solution(17449967668425388429)
XLA Ops:
  0.6 0.7 %shard_map.77.refs_0_.packed = f32[9,256]{1,0:T(8,128)S(1)} custom-call(f32[8,256]{1,0:T(8,128)} %rhs.1, f32[1,256]{1,0:T(1,128)} %bitcast.1), custom_call_target="tpu_custom_call" | custom-call | tf_op jit(solution)/shard_map/pallas_call | solution.py:205
  1.4 2.5 %collective-permute-start.2 = (f32[9,256]{1,0:T(8,128)S(1)}, f32[9,256]{1,0:T(8,128)S(1)}, u32[]{:S(2)}, u32[]{:S(2)}) collective-permute-start(f32[9,256]{1,0:T(8,128)S(1)} %shard_map.77.refs_0_.packed), channel_id=1, source_target_pairs={{0,24},{8,16},{16,8},{24,0},{1,25},{9,17},{17,9},{25,1},{2,26},{10... | collective-permute-start | bytes 27656 | tf_op jit(solution)/shard_map/ppermute | solution.py:232
  3.9 0.6 %collective-permute-start.1 = (f32[9,256]{1,0:T(8,128)S(1)}, f32[9,256]{1,0:T(8,128)S(1)}, u32[]{:S(2)}, u32[]{:S(2)}) collective-permute-start(f32[9,256]{1,0:T(8,128)S(1)} %shard_map.77.refs_0_.packed), channel_id=1, source_target_pairs={{0,16},{8,24},{16,0},{24,8},{1,17},{9,25},{17,1},{25,9},{2,18},{10... | collective-permute-start | bytes 27656 | tf_op jit(solution)/shard_map/ppermute | solution.py:232
  4.5 0.0 collective-permute-start
  5.2 1.0 %shard_map.78 = (bf16[8,128,128]{2,1,0:T(8,128)(2,1)S(1)}, s32[8,8,128]{2,1,0:T(8,128)S(1)}, s32[8,8,128]{2,1,0:T(8,128)S(1)}) custom-call(s32[1,1,8]{2,1,0:T(1,128)} %cols.1, s32[1,1,8]{2,1,0:T(1,128)} %offsets.1, s32[1,1,1]{2,1,0:T(1,128)S(6)} %copy.8.count, bf16[1,1,8,128,128]{4,3,2,1,0:T(8,128)(2,1)} %tiles.1), custom_call_target="tpu_custom_call" | custom-call | bytes 4194304 | tf_op jit(solution)/shard_map/pallas_call | solution.py:216
  6.2 0.0 collective-permute-done.2.refs_3_
  6.2 1.4 %collective-permute-done.1.refs_2_ = f32[9,256]{1,0:T(8,128)S(1)} collective-permute-done((f32[9,256]{1,0:T(8,128)S(1)}, f32[9,256]{1,0:T(8,128)S(1)}, u32[]{:S(2)}, u32[]{:S(2)}) %collective-permute-start.1) | collective-permute-done | bytes 9248 | tf_op jit(solution)/shard_map/ppermute | solution.py:232
  7.6 0.0 collective-permute-done.refs_1_
  7.6 0.3 shard_map.79
  7.9 12.2 %all_to_all.15.refs_6_.refs_7_.where = bf16[32,5,2,128]{3,2,1,0:T(2,128)(2,1)S(1)} all-to-all(bf16[32,5,2,128]{3,2,1,0:T(2,128)(2,1)S(1)} %shard_map.79), channel_id=1, replica_groups=mesh['row'=4,'col'=8] {'row','col'}, dimensions={0} | all-to-all | bytes 163840 | tf_op jit(solution)/shard_map/all_to_all | solution.py:200
  20.1 0.3 shard_map.80
  20.4 9.0 %all_to_all.16.refs_7_ = bf16[32,8,128]{2,1,0:T(8,128)(2,1)S(1)} all-to-all(bf16[32,8,128]{2,1,0:T(8,128)(2,1)S(1)} %get-tuple-element.16), channel_id=1, replica_groups=mesh['row'=4,'col'=8] {'row','col'}, dimensions={0} | all-to-all | bytes 131072 | tf_op jit(solution)/shard_map/all_to_all | solution.py:200
  29.4 0.3 shard_map.81
  29.6 9.0 %all_to_all.17.moved = bf16[8,8,128]{2,1,0:T(8,128)(2,1)S(1)} all-to-all(bf16[8,8,128]{2,1,0:T(8,128)(2,1)S(1)} %get-tuple-element.20), channel_id=1, replica_groups=mesh['row'=4,'col'=8] {'col'}, dimensions={0} | all-to-all | bytes 32768 | tf_op jit(solution)/shard_map/all_to_all | solution.py:200
  38.6 0.6 %shard_map.82 = (f32[8,256]{1,0:T(8,128)}, f32[8,256]{1,0:T(8,128)}) custom-call(f32[9,256]{1,0:T(8,128)S(1)} %shard_map.77.refs_0_.packed, bf16[32,5,2,128]{3,2,1,0:T(2,128)(2,1)S(1)} %all_to_all.15.refs_6_.refs_7_.where, bf16[8,8,128]{2,1,0:T(8,128)(2,1)S(1)} %all_to_all.17.moved, f32[8,8,128]{2,1,0:T(8,128)S(1)} %get-tuple-element.21.old_dir, ...), custom_call_target="tpu_custom_call" | custom-call | tf_op jit(solution)/shard_map/pallas_call | solution.py:253
Async XLA Ops:
  1.4 4.8 %collective-permute-start.2 = (f32[9,256]{1,0:T(8,128)S(1)}, f32[9,256]{1,0:T(8,128)S(1)}, u32[]{:S(2)}, u32[]{:S(2)}) collective-permute-start(f32[9,256]{1,0:T(8,128)S(1)} %shard_map.77.refs_0_.packed), channel_id=1, source_target_pairs={{0,24},{8,16},{16,8},{24,0},{1,25},{9,17},{17,9},{25,1},{2,26},{10... | collective-permute-start | bytes 27656 | tf_op jit(solution)/shard_map/ppermute | solution.py:232
  3.9 3.7 %collective-permute-start.1 = (f32[9,256]{1,0:T(8,128)S(1)}, f32[9,256]{1,0:T(8,128)S(1)}, u32[]{:S(2)}, u32[]{:S(2)}) collective-permute-start(f32[9,256]{1,0:T(8,128)S(1)} %shard_map.77.refs_0_.packed), channel_id=1, source_target_pairs={{0,16},{8,24},{16,0},{24,8},{1,17},{9,25},{17,1},{25,9},{2,18},{10... | collective-permute-start | bytes 27656 | tf_op jit(solution)/shard_map/ppermute | solution.py:232
  4.5 3.1 %collective-permute-start = (f32[9,256]{1,0:T(8,128)S(1)}, f32[9,256]{1,0:T(8,128)S(1)}, u32[]{:S(2)}, u32[]{:S(2)}) collective-permute-start(f32[9,256]{1,0:T(8,128)S(1)} %shard_map.77.refs_0_.packed), channel_id=1, source_target_pairs={{0,8},{8,0},{16,24},{24,16},{1,9},{9,1},{17,25},{25,17},{2,10},{10... | collective-permute-start | bytes 27656 | tf_op jit(solution)/shard_map/ppermute | solution.py:232

commit v5 on v4

--- a/solution.py
+++ b/solution.py
@@ -64,6 +64,11 @@
     copies[2].wait()
 
 
+def column_order(ncol):
+    middle = ncol // 2 - 1
+    return [middle] + [c for c in range(ncol) if c != middle]
+
+
 def multiply(directions, tiles, column, out, rows, ncol, offset=None):
     slots = tiles.shape[0]
     samples = column.shape[1]
@@ -81,6 +86,8 @@
         first = (t // ncol) * samples
         for r in range(rows):
             place = r * ncol + t % ncol
+            if rows == 1:
+                place = column_order(ncol).index(t % ncol)
             if offset is None:
                 out[place, pl.ds(first, samples), :] = sent
             else:
@@ -97,7 +104,7 @@
     return rhs, diag
 
 
-def coupled(moved, where, r, ncol, share, samples, piece, base=None):
+def coupled(moved, where, r, ncol, share, samples, piece, last=False):
     totals = [None] * piece
     pairs = samples // PAIR
     for c in range(ncol):
@@ -108,7 +115,7 @@
             if moved is where:
                 term = moved[place, pl.ds(first, pairs)].reshape(samples, off.shape[1])
             else:
-                here = place if base is None else base + c
+                here = place if not last else column_order(ncol).index(c)
                 term = moved[here, pl.ds(a * samples, samples), :]
             term = term.astype(jnp.float32)
             for k in range(piece):
@@ -169,7 +176,7 @@
     rows, ncol, piece, width = dims
     samples = packed.shape[0] - 1
     me = lax.axis_index("row")
-    image = coupled(moved, where, me, ncol, share, samples, piece, 0)
+    image = coupled(moved, where, me, ncol, share, samples, piece, True)
     for k in range(piece):
         lanes = slice(k * width, (k + 1) * width)
         diag = packed[samples : samples + 1, lanes]
@@ -196,8 +203,13 @@
     )
     params = pltpu.CompilerParams(vmem_limit_bytes=VMEM_BYTES)
 
-    def exchange(x, axes=("row", "col")):
-        return lax.all_to_all(x, axes, split_axis=0, concat_axis=0, tiled=True)
+    def exchange(x):
+        return lax.all_to_all(x, ("row", "col"), split_axis=0, concat_axis=0, tiled=True)
+
+    def exchange_columns(x):
+        return lax.all_to_all(
+            x, "col", 0, 0, axis_index_groups=[column_order(ncol)], tiled=True
+        )
 
     def far(x):
         return pltpu.with_memory_space_constraint(x, pltpu.HBM)
@@ -248,7 +260,7 @@
             out_specs=(vmem,) * 4,
             compiler_params=params,
         )(*pieces, held, column, where, moved, *states)
-        moved = exchange(sent, ("row", "col") if step + 2 < STEPS else "col")
+        moved = exchange(sent) if step + 2 < STEPS else exchange_columns(sent)
     out = jax.ShapeDtypeStruct(rhs.shape, jnp.float32)
     return pl.pallas_call(
         functools.partial(last_kernel, dims, share),

time: 39.5 us -> 38.7 us (0.980)
  blocking collectives: 30.1 us -> 29.4 us
    all_to_all x3, blocking collectives: 30.1 us -> 29.4 us  [the longest x2 21.2 us: exchange(): lax.all_to_all(x, ('row', 'col'), split_axis=0, concat_axis=0, tiled=True)]
where the time goes in v5:
time: 38.7 us; the launch traced here: 38.4 us
  blocking collectives  29.4 us (76%)
  Pallas kernels  3.18 us (8%)
  starting transfers between devices  3.18 us (8%)
  waiting for transfers between devices  1.41 us (4%)
  between operations  1.32 us (3%)
    all_to_all x2, blocking collectives, exchange(): lax.all_to_all(x, ('row', 'col'), split_axis=0, concat_axis=0, tiled=True)  21.2 us
    all_to_all x1, blocking collectives, exchange_columns(): lax.all_to_all(x, 'col', 0, 0, axis_index_groups=[column_order(ncol)], ti...  8.19 us
    ppermute x3, starting transfers between devices, body(): pieces[p] = lax.ppermute(packed, 'row', [(i, i ^ p) for i in range(rows)])  3.18 us
    ppermute x3, waiting for transfers between devices, body(): pieces[p] = lax.ppermute(packed, 'row', [(i, i ^ p) for i in range(rows)])  1.41 us
    pallas_call x1, Pallas kernels, body(): pl.pallas_call(functools.partial(prep_kernel, piece), out_shape=(jax.Shap...  0.98 us
  transfers between devices with their start and end apart: 3, of which 1 were waited for; matrix products, arithmetic and copies ran while one was open for 0% of the time, Pallas kernels for 3%

profile of v5, /device:TPU:0, one launch (start us, length us, event | category | flops | bytes accessed | tf_op | source)
XLA Modules:
  0.0 38.4 jit_solution(4320682171116759799)
XLA Ops:
  0.6 0.7 %shard_map.77.refs_0_.packed = f32[9,256]{1,0:T(8,128)S(1)} custom-call(f32[8,256]{1,0:T(8,128)} %rhs.1, f32[1,256]{1,0:T(1,128)} %bitcast.1), custom_call_target="tpu_custom_call" | custom-call | tf_op jit(solution)/shard_map/pallas_call | solution.py:217
  1.4 2.5 %collective-permute-start.2 = (f32[9,256]{1,0:T(8,128)S(1)}, f32[9,256]{1,0:T(8,128)S(1)}, u32[]{:S(2)}, u32[]{:S(2)}) collective-permute-start(f32[9,256]{1,0:T(8,128)S(1)} %shard_map.77.refs_0_.packed), channel_id=1, source_target_pairs={{0,24},{8,16},{16,8},{24,0},{1,25},{9,17},{17,9},{25,1},{2,26},{10... | collective-permute-start | bytes 27656 | tf_op jit(solution)/shard_map/ppermute | solution.py:244
  3.9 0.6 %collective-permute-start.1 = (f32[9,256]{1,0:T(8,128)S(1)}, f32[9,256]{1,0:T(8,128)S(1)}, u32[]{:S(2)}, u32[]{:S(2)}) collective-permute-start(f32[9,256]{1,0:T(8,128)S(1)} %shard_map.77.refs_0_.packed), channel_id=1, source_target_pairs={{0,16},{8,24},{16,0},{24,8},{1,17},{9,25},{17,1},{25,9},{2,18},{10... | collective-permute-start | bytes 27656 | tf_op jit(solution)/shard_map/ppermute | solution.py:244
  4.5 0.0 collective-permute-start
  5.2 1.0 %shard_map.78 = (bf16[8,128,128]{2,1,0:T(8,128)(2,1)S(1)}, s32[8,8,128]{2,1,0:T(8,128)S(1)}, s32[8,8,128]{2,1,0:T(8,128)S(1)}) custom-call(s32[1,1,8]{2,1,0:T(1,128)} %cols.1, s32[1,1,8]{2,1,0:T(1,128)} %offsets.1, s32[1,1,1]{2,1,0:T(1,128)S(6)} %copy.8.count, bf16[1,1,8,128,128]{4,3,2,1,0:T(8,128)(2,1)} %tiles.1), custom_call_target="tpu_custom_call" | custom-call | bytes 4194304 | tf_op jit(solution)/shard_map/pallas_call | solution.py:228
  6.2 0.0 collective-permute-done.2.refs_3_
  6.2 1.4 %collective-permute-done.1.refs_2_ = f32[9,256]{1,0:T(8,128)S(1)} collective-permute-done((f32[9,256]{1,0:T(8,128)S(1)}, f32[9,256]{1,0:T(8,128)S(1)}, u32[]{:S(2)}, u32[]{:S(2)}) %collective-permute-start.1) | collective-permute-done | bytes 9248 | tf_op jit(solution)/shard_map/ppermute | solution.py:244
  7.6 0.0 collective-permute-done.refs_1_
  7.6 0.3 shard_map.79
  7.9 12.2 %all_to_all.15.refs_6_.refs_7_.where = bf16[32,5,2,128]{3,2,1,0:T(2,128)(2,1)S(1)} all-to-all(bf16[32,5,2,128]{3,2,1,0:T(2,128)(2,1)S(1)} %shard_map.79), channel_id=1, replica_groups=mesh['row'=4,'col'=8] {'row','col'}, dimensions={0} | all-to-all | bytes 163840 | tf_op jit(solution)/shard_map/all_to_all | solution.py:207
  20.1 0.3 shard_map.80
  20.4 9.0 %all_to_all.16.refs_7_ = bf16[32,8,128]{2,1,0:T(8,128)(2,1)S(1)} all-to-all(bf16[32,8,128]{2,1,0:T(8,128)(2,1)S(1)} %get-tuple-element.16), channel_id=1, replica_groups=mesh['row'=4,'col'=8] {'row','col'}, dimensions={0} | all-to-all | bytes 131072 | tf_op jit(solution)/shard_map/all_to_all | solution.py:207
  29.4 0.3 shard_map.81
  29.6 8.2 %all_to_all.17.moved = bf16[8,8,128]{2,1,0:T(8,128)(2,1)S(1)} all-to-all(bf16[8,8,128]{2,1,0:T(8,128)(2,1)S(1)} %get-tuple-element.20), channel_id=1, replica_groups={{3,0,1,2,4,5,6,7},{11,8,9,10,12,13,14,15},{19,16,17,18,20,21,22,23},{27..., dimensions={0} | all-to-all | bytes 32768 | tf_op jit(solution)/shard_map/all_to_all | solution.py:210
  37.8 0.6 %shard_map.82 = (f32[8,256]{1,0:T(8,128)}, f32[8,256]{1,0:T(8,128)}) custom-call(f32[9,256]{1,0:T(8,128)S(1)} %shard_map.77.refs_0_.packed, bf16[32,5,2,128]{3,2,1,0:T(2,128)(2,1)S(1)} %all_to_all.15.refs_6_.refs_7_.where, bf16[8,8,128]{2,1,0:T(8,128)(2,1)S(1)} %all_to_all.17.moved, f32[8,8,128]{2,1,0:T(8,128)S(1)} %get-tuple-element.21.old_dir, ...), custom_call_target="tpu_custom_call" | custom-call | tf_op jit(solution)/shard_map/pallas_call | solution.py:265
Async XLA Ops:
  1.4 4.8 %collective-permute-start.2 = (f32[9,256]{1,0:T(8,128)S(1)}, f32[9,256]{1,0:T(8,128)S(1)}, u32[]{:S(2)}, u32[]{:S(2)}) collective-permute-start(f32[9,256]{1,0:T(8,128)S(1)} %shard_map.77.refs_0_.packed), channel_id=1, source_target_pairs={{0,24},{8,16},{16,8},{24,0},{1,25},{9,17},{17,9},{25,1},{2,26},{10... | collective-permute-start | bytes 27656 | tf_op jit(solution)/shard_map/ppermute | solution.py:244
  3.9 3.7 %collective-permute-start.1 = (f32[9,256]{1,0:T(8,128)S(1)}, f32[9,256]{1,0:T(8,128)S(1)}, u32[]{:S(2)}, u32[]{:S(2)}) collective-permute-start(f32[9,256]{1,0:T(8,128)S(1)} %shard_map.77.refs_0_.packed), channel_id=1, source_target_pairs={{0,16},{8,24},{16,0},{24,8},{1,17},{9,25},{17,1},{25,9},{2,18},{10... | collective-permute-start | bytes 27656 | tf_op jit(solution)/shard_map/ppermute | solution.py:244
  4.5 3.1 %collective-permute-start = (f32[9,256]{1,0:T(8,128)S(1)}, f32[9,256]{1,0:T(8,128)S(1)}, u32[]{:S(2)}, u32[]{:S(2)}) collective-permute-start(f32[9,256]{1,0:T(8,128)S(1)} %shard_map.77.refs_0_.packed), channel_id=1, source_target_pairs={{0,8},{8,0},{16,24},{24,16},{1,9},{9,1},{17,25},{25,17},{2,10},{10... | collective-permute-start | bytes 27656 | tf_op jit(solution)/shard_map/ppermute | solution.py:244

commit v6 on v5

--- a/solution.py
+++ b/solution.py
@@ -10,6 +10,7 @@
 STEPS = 3
 VMEM_BYTES = 16 << 20
 PAIR = 2
+GROUP = 2
 
 lower_bound = 0.3
 upper_bound = 1.9
@@ -45,11 +46,14 @@
 def prep_kernel(piece, cols, offsets, count, tiles, held, column, offset, *scratch):
     cols_here, offsets_here, sems = scratch
     me = lax.axis_index("row")
+    slots, width = tiles.shape[2:4]
+    pairs = [(cols, cols_here), (offsets, offsets_here)]
+    for t in range(slots):
+        lanes = pl.ds(t % GROUP * width, width)
+        pairs.append((tiles.at[0, 0, t], held.at[t // GROUP, :, lanes]))
     copies = [
         pltpu.make_async_copy(source, target, sems.at[i])
-        for i, (source, target) in enumerate(
-            [(cols, cols_here), (offsets, offsets_here), (tiles.at[0, 0], held)]
-        )
+        for i, (source, target) in enumerate(pairs)
     ]
     for copy in copies:
         copy.start()
@@ -61,40 +65,49 @@
         here = jnp.where(t < count[0, 0, 0], col, -1)
         column[t] = jnp.full(column.shape[1:], here, jnp.int32)
         offset[t] = jnp.full(offset.shape[1:], offsets_here[0, 0, t], jnp.int32)
-    copies[2].wait()
+    for copy in copies[2:]:
+        copy.wait()
 
 
 def column_order(ncol):
-    middle = ncol // 2 - 1
-    return [middle] + [c for c in range(ncol) if c != middle]
+    half = ncol // 2
+    return list(range(half))[::-1] + list(range(half, ncol))[::-1]
 
 
 def multiply(directions, tiles, column, out, rows, ncol, offset=None):
-    slots = tiles.shape[0]
-    samples = column.shape[1]
-    for t in range(slots):
-        where = column[t]
-        picked = jnp.zeros_like(directions[0])
-        for j, direction in enumerate(directions):
-            picked = jnp.where(where == j, direction, picked)
+    slots, samples, width = column.shape
+    order = column_order(ncol) if rows == 1 else list(range(ncol))
+    blank = jnp.zeros((samples, width), jnp.bfloat16)
+    for first in range(0, slots, GROUP):
+        lines = []
+        for g in range(GROUP):
+            where = column[first + g]
+            picked = jnp.zeros_like(directions[0])
+            for j, direction in enumerate(directions):
+                picked = jnp.where(where == j, direction, picked)
+            picked = picked.astype(jnp.bfloat16)
+            line = [picked if h == g else blank for h in range(GROUP)]
+            lines.append(jnp.concatenate(line, axis=1))
         sent = lax.dot_general(
-            picked.astype(jnp.bfloat16),
-            tiles[t],
+            jnp.concatenate(lines, axis=0),
+            tiles[first // GROUP],
             (((1,), (1,)), ((), ())),
             preferred_element_type=jnp.float32,
-        ).astype(jnp.bfloat16)
-        first = (t // ncol) * samples
-        for r in range(rows):
-            place = r * ncol + t % ncol
-            if rows == 1:
-                place = column_order(ncol).index(t % ncol)
-            if offset is None:
-                out[place, pl.ds(first, samples), :] = sent
-            else:
-                pairs = samples // PAIR
-                first = (t // ncol) * (pairs + 1)
-                out[place, pl.ds(first, pairs)] = sent.reshape(pairs, PAIR, sent.shape[1])
-                out[place, first + pairs] = offset[t][:PAIR].astype(jnp.float32).astype(jnp.bfloat16)
+        )
+        for g in range(GROUP):
+            t = first + g
+            mine = sent[g * samples : (g + 1) * samples].astype(jnp.bfloat16)
+            for r in range(rows):
+                place = r * ncol + order.index(t % ncol)
+                if offset is None:
+                    out[place, pl.ds((t // ncol) * samples, samples), :] = mine
+                else:
+                    pairs = samples // PAIR
+                    begin = (t // ncol) * (pairs + 1)
+                    out[place, pl.ds(begin, pairs)] = mine.reshape(pairs, PAIR, width)
+                    out[place, begin + pairs] = (
+                        offset[t][:PAIR].astype(jnp.float32).astype(jnp.bfloat16)
+                    )
 
 
 def part(packed, k, width):
@@ -104,19 +117,23 @@
     return rhs, diag
 
 
-def coupled(moved, where, r, ncol, share, samples, piece, last=False):
+def coupled(moved, where, r, ncol, share, samples, piece, kept=None, last=False):
     totals = [None] * piece
     pairs = samples // PAIR
+    order = column_order(ncol)
     for c in range(ncol):
         for a in range(share):
             place = r * ncol + c
-            first = a * (pairs + 1)
-            off = where[place, first + pairs].astype(jnp.float32)[:1]
-            if moved is where:
-                term = moved[place, pl.ds(first, pairs)].reshape(samples, off.shape[1])
+            if kept is not None:
+                first = a * (pairs + 1)
+                term = moved[place, pl.ds(first, pairs)].reshape(samples, moved.shape[3])
+                off = moved[place, first + pairs].astype(jnp.float32)[:1]
+                off = jnp.broadcast_to(off, term.shape)
+                kept[place * share + a] = off
             else:
-                here = place if not last else column_order(ncol).index(c)
+                here = order.index(c) if last else place
                 term = moved[here, pl.ds(a * samples, samples), :]
+                off = where[place * share + a]
             term = term.astype(jnp.float32)
             for k in range(piece):
                 mine = jnp.where(off == k, term, 0.0)
@@ -139,20 +156,19 @@
 def middle_kernel(dims, step, *refs):
     rows, ncol, piece, width = dims
     packed = refs[:rows]
-    tiles, column, where, moved = refs[rows : rows + 4]
+    tiles, column, moved = refs[rows : rows + 3]
+    samples = packed[0].shape[0] - 1
+    share = column.shape[0] // ncol
+    a, b = coefficients()[step]
+    where = kept = None
     if step == 0:
-        moved = where
-    samples = packed[0].shape[0] - 1
-    share = tiles.shape[0] // ncol
-    a, b = coefficients()[step]
-    if step == 0:
-        out, new_dir, new_res, new_sol = refs[rows + 4 :]
+        out, new_dir, new_res, new_sol, kept = refs[rows + 3 :]
     else:
-        old_dir, old_res, old_sol, out, new_dir, new_res, new_sol = refs[rows + 4 :]
+        where, old_dir, old_res, old_sol, out, new_dir, new_res, new_sol = refs[rows + 3 :]
     me = lax.axis_index("row")
     directions = []
     for p in range(rows):
-        image = coupled(moved, where, me ^ p, ncol, share, samples, piece)
+        image = coupled(moved, where, me ^ p, ncol, share, samples, piece, kept)
         for k in range(piece):
             rhs, diag = part(packed[p], k, width)
             inverse = 1.0 / diag
@@ -176,7 +192,7 @@
     rows, ncol, piece, width = dims
     samples = packed.shape[0] - 1
     me = lax.axis_index("row")
-    image = coupled(moved, where, me, ncol, share, samples, piece, True)
+    image = coupled(moved, where, me, ncol, share, samples, piece, last=True)
     for k in range(piece):
         lanes = slice(k * width, (k + 1) * width)
         diag = packed[samples : samples + 1, lanes]
@@ -195,6 +211,8 @@
     vmem = pl.BlockSpec(memory_space=pltpu.VMEM)
     hbm = pl.BlockSpec(memory_space=pltpu.HBM)
     state = jax.ShapeDtypeStruct((blocks, samples, width), jnp.float32)
+    grouped = jax.ShapeDtypeStruct((slots // GROUP, width, GROUP * width), tiles.dtype)
+    kept = jax.ShapeDtypeStruct((rows * ncol * share, samples, width), jnp.float32)
     table = jax.ShapeDtypeStruct((slots, samples, width), jnp.int32)
     narrow = jax.ShapeDtypeStruct((ncol, share * samples, width), jnp.bfloat16)
     message = jax.ShapeDtypeStruct((rows * ncol, share * samples, width), jnp.bfloat16)
@@ -227,13 +245,13 @@
     )(far(rhs), far(stiff_diag[None, :]))
     held, column, offset = pl.pallas_call(
         functools.partial(prep_kernel, piece),
-        out_shape=(jax.ShapeDtypeStruct(tiles.shape[2:], tiles.dtype), table, table),
+        out_shape=(grouped, table, table),
         in_specs=[hbm] * 2 + [pl.BlockSpec(memory_space=pltpu.SMEM)] + [hbm],
         out_specs=(vmem,) * 3,
         scratch_shapes=[
             pltpu.SMEM(tile_cols.shape, jnp.int32),
             pltpu.SMEM(tile_offsets.shape, jnp.int32),
-            pltpu.SemaphoreType.DMA((3,)),
+            pltpu.SemaphoreType.DMA((slots + 2,)),
         ],
         compiler_params=params,
         cost_estimate=pl.CostEstimate(flops=0, bytes_accessed=4 << 20, transcendentals=0),
@@ -250,25 +268,32 @@
         out_specs=vmem,
         compiler_params=params,
     )(*pieces, held, column, offset)
-    moved = where = exchange(sent)
-    states = ()
+    moved = exchange(sent)
+    states = []
     for step in range(STEPS - 1):
-        sent, *states = pl.pallas_call(
+        shapes = [message if step + 2 < STEPS else narrow, state, state, state]
+        if step == 0:
+            shapes.append(kept)
+        results = pl.pallas_call(
             functools.partial(middle_kernel, dims, step),
-            out_shape=(message if step + 2 < STEPS else narrow, state, state, state),
-            in_specs=[vmem] * (rows + 4 + len(states)),
-            out_specs=(vmem,) * 4,
+            out_shape=shapes,
+            in_specs=[vmem] * (rows + 3 + len(states)),
+            out_specs=[vmem] * len(shapes),
             compiler_params=params,
-        )(*pieces, held, column, where, moved, *states)
+        )(*pieces, held, column, moved, *states)
+        sent = results[0]
+        if step == 0:
+            where = results[4]
+        states = [where, *results[1:4]]
         moved = exchange(sent) if step + 2 < STEPS else exchange_columns(sent)
     out = jax.ShapeDtypeStruct(rhs.shape, jnp.float32)
     return pl.pallas_call(
         functools.partial(last_kernel, dims, share),
         out_shape=(out, out),
-        in_specs=[vmem] * (3 + len(states)),
+        in_specs=[vmem] * 6,
         out_specs=(vmem, vmem),
         compiler_params=params,
-    )(packed, where, moved, *states)
+    )(packed, where, moved, *states[1:])
 
 
 def solution(mesh):

time: 38.7 us -> 38.5 us (level)
  no operation moved by 1% of the time
where the time goes in v6:
time: 38.5 us; the launch traced here: 38.2 us
  blocking collectives  29.3 us (76%)
  starting transfers between devices  3.18 us (8%)
  Pallas kernels  2.94 us (8%)
  waiting for transfers between devices  1.43 us (4%)
  between operations  1.32 us (3%)
    all_to_all x2, blocking collectives, exchange(): lax.all_to_all(x, ('row', 'col'), split_axis=0, concat_axis=0, tiled=True)  21.2 us
    all_to_all x1, blocking collectives, exchange_columns(): lax.all_to_all(x, 'col', 0, 0, axis_index_groups=[column_order(ncol)], ti...  8.15 us
    ppermute x3, starting transfers between devices, body(): pieces[p] = lax.ppermute(packed, 'row', [(i, i ^ p) for i in range(rows)])  3.18 us
    ppermute x3, waiting for transfers between devices, body(): pieces[p] = lax.ppermute(packed, 'row', [(i, i ^ p) for i in range(rows)])  1.43 us
    pallas_call x1, Pallas kernels, body(): pl.pallas_call(functools.partial(prep_kernel, piece), out_shape=(grouped,...  0.97 us
  transfers between devices with their start and end apart: 3, of which 1 were waited for; matrix products, arithmetic and copies ran while one was open for 0% of the time, Pallas kernels for 3%

profile of v6, /device:TPU:0, one launch (start us, length us, event | category | flops | bytes accessed | tf_op | source)
XLA Modules:
  0.0 38.2 jit_solution(10814070339718086767)
XLA Ops:
  0.6 0.7 %shard_map.77.refs_0_.packed = f32[9,256]{1,0:T(8,128)S(1)} custom-call(f32[8,256]{1,0:T(8,128)} %rhs.1, f32[1,256]{1,0:T(1,128)} %bitcast.1), custom_call_target="tpu_custom_call" | custom-call | tf_op jit(solution)/shard_map/pallas_call | solution.py:235
  1.4 2.5 %collective-permute-start.2 = (f32[9,256]{1,0:T(8,128)S(1)}, f32[9,256]{1,0:T(8,128)S(1)}, u32[]{:S(2)}, u32[]{:S(2)}) collective-permute-start(f32[9,256]{1,0:T(8,128)S(1)} %shard_map.77.refs_0_.packed), channel_id=1, source_target_pairs={{0,24},{8,16},{16,8},{24,0},{1,25},{9,17},{17,9},{25,1},{2,26},{10... | collective-permute-start | bytes 27656 | tf_op jit(solution)/shard_map/ppermute | solution.py:262
  3.9 0.6 %collective-permute-start.1 = (f32[9,256]{1,0:T(8,128)S(1)}, f32[9,256]{1,0:T(8,128)S(1)}, u32[]{:S(2)}, u32[]{:S(2)}) collective-permute-start(f32[9,256]{1,0:T(8,128)S(1)} %shard_map.77.refs_0_.packed), channel_id=1, source_target_pairs={{0,16},{8,24},{16,0},{24,8},{1,17},{9,25},{17,1},{25,9},{2,18},{10... | collective-permute-start | bytes 27656 | tf_op jit(solution)/shard_map/ppermute | solution.py:262
  4.5 0.0 collective-permute-start
  5.2 1.0 %shard_map.78 = (bf16[4,128,256]{2,1,0:T(8,128)(2,1)S(1)}, s32[8,8,128]{2,1,0:T(8,128)S(1)}, s32[8,8,128]{2,1,0:T(8,128)S(1)}) custom-call(s32[1,1,8]{2,1,0:T(1,128)} %cols.1, s32[1,1,8]{2,1,0:T(1,128)} %offsets.1, s32[1,1,1]{2,1,0:T(1,128)S(6)} %copy.8.count, bf16[1,1,8,128,128]{4,3,2,1,0:T(8,128)(2,1)} %tiles.1), custom_call_target="tpu_custom_call" | custom-call | bytes 4194304 | tf_op jit(solution)/shard_map/pallas_call | solution.py:246
  6.2 0.0 collective-permute-done.2.refs_3_
  6.2 1.4 %collective-permute-done.1.refs_2_ = f32[9,256]{1,0:T(8,128)S(1)} collective-permute-done((f32[9,256]{1,0:T(8,128)S(1)}, f32[9,256]{1,0:T(8,128)S(1)}, u32[]{:S(2)}, u32[]{:S(2)}) %collective-permute-start.1) | collective-permute-done | bytes 9248 | tf_op jit(solution)/shard_map/ppermute | solution.py:262
  7.6 0.0 collective-permute-done.refs_1_
  7.6 0.2 shard_map.79
  7.8 12.2 %all_to_all.15.refs_6_ = bf16[32,5,2,128]{3,2,1,0:T(2,128)(2,1)S(1)} all-to-all(bf16[32,5,2,128]{3,2,1,0:T(2,128)(2,1)S(1)} %shard_map.79), channel_id=1, replica_groups=mesh['row'=4,'col'=8] {'row','col'}, dimensions={0} | all-to-all | bytes 163840 | tf_op jit(solution)/shard_map/all_to_all | solution.py:225
  20.0 0.2 shard_map.80
  20.2 9.0 %all_to_all.16.refs_6_ = bf16[32,8,128]{2,1,0:T(8,128)(2,1)S(1)} all-to-all(bf16[32,8,128]{2,1,0:T(8,128)(2,1)S(1)} %get-tuple-element.18), channel_id=1, replica_groups=mesh['row'=4,'col'=8] {'row','col'}, dimensions={0} | all-to-all | bytes 131072 | tf_op jit(solution)/shard_map/all_to_all | solution.py:225
  29.2 0.2 shard_map.81
  29.4 8.2 %all_to_all.17.moved = bf16[8,8,128]{2,1,0:T(8,128)(2,1)S(1)} all-to-all(bf16[8,8,128]{2,1,0:T(8,128)(2,1)S(1)} %get-tuple-element.22), channel_id=1, replica_groups={{3,2,1,0,7,6,5,4},{11,10,9,8,15,14,13,12},{19,18,17,16,23,22,21,20},{27..., dimensions={0} | all-to-all | bytes 32768 | tf_op jit(solution)/shard_map/all_to_all | solution.py:228
  37.6 0.6 %shard_map.82 = (f32[8,256]{1,0:T(8,128)}, f32[8,256]{1,0:T(8,128)}) custom-call(f32[9,256]{1,0:T(8,128)S(1)} %shard_map.77.refs_0_.packed, f32[32,8,128]{2,1,0:T(8,128)S(1)} %get-tuple-element.17.refs_7_.where, bf16[8,8,128]{2,1,0:T(8,128)(2,1)S(1)} %all_to_all.17.moved, f32[8,8,128]{2,1,0:T(8,128)S(1)} %get-tuple-element.23.old_dir, ...), custom_call_target="tpu_custom_call" | custom-call | tf_op jit(solution)/shard_map/pallas_call | solution.py:290
Async XLA Ops:
  1.4 4.8 %collective-permute-start.2 = (f32[9,256]{1,0:T(8,128)S(1)}, f32[9,256]{1,0:T(8,128)S(1)}, u32[]{:S(2)}, u32[]{:S(2)}) collective-permute-start(f32[9,256]{1,0:T(8,128)S(1)} %shard_map.77.refs_0_.packed), channel_id=1, source_target_pairs={{0,24},{8,16},{16,8},{24,0},{1,25},{9,17},{17,9},{25,1},{2,26},{10... | collective-permute-start | bytes 27656 | tf_op jit(solution)/shard_map/ppermute | solution.py:262
  3.9 3.7 %collective-permute-start.1 = (f32[9,256]{1,0:T(8,128)S(1)}, f32[9,256]{1,0:T(8,128)S(1)}, u32[]{:S(2)}, u32[]{:S(2)}) collective-permute-start(f32[9,256]{1,0:T(8,128)S(1)} %shard_map.77.refs_0_.packed), channel_id=1, source_target_pairs={{0,16},{8,24},{16,0},{24,8},{1,17},{9,25},{17,1},{25,9},{2,18},{10... | collective-permute-start | bytes 27656 | tf_op jit(solution)/shard_map/ppermute | solution.py:262
  4.5 3.1 %collective-permute-start = (f32[9,256]{1,0:T(8,128)S(1)}, f32[9,256]{1,0:T(8,128)S(1)}, u32[]{:S(2)}, u32[]{:S(2)}) collective-permute-start(f32[9,256]{1,0:T(8,128)S(1)} %shard_map.77.refs_0_.packed), channel_id=1, source_target_pairs={{0,8},{8,0},{16,24},{24,16},{1,9},{9,1},{17,25},{25,17},{2,10},{10... | collective-permute-start | bytes 27656 | tf_op jit(solution)/shard_map/ppermute | solution.py:262

commit v7 on v6

--- a/solution.py
+++ b/solution.py
@@ -1,4 +1,5 @@
 import functools
+import math
 
 import jax
 import jax.numpy as jnp
@@ -69,6 +70,11 @@
         copy.wait()
 
 
+def stride(rows, ncol):
+    n = rows * ncol
+    return n - 13 if n > 13 and math.gcd(n, 13) == 1 else 1
+
+
 def column_order(ncol):
     half = ncol // 2
     return list(range(half))[::-1] + list(range(half, ncol))[::-1]
@@ -76,7 +82,7 @@
 
 def multiply(directions, tiles, column, out, rows, ncol, offset=None):
     slots, samples, width = column.shape
-    order = column_order(ncol) if rows == 1 else list(range(ncol))
+    order = column_order(ncol)
     blank = jnp.zeros((samples, width), jnp.bfloat16)
     for first in range(0, slots, GROUP):
         lines = []
@@ -98,7 +104,9 @@
             t = first + g
             mine = sent[g * samples : (g + 1) * samples].astype(jnp.bfloat16)
             for r in range(rows):
-                place = r * ncol + order.index(t % ncol)
+                place = stride(rows, ncol) * (r * ncol + t % ncol) % (rows * ncol)
+                if rows == 1:
+                    place = order.index(t % ncol)
                 if offset is None:
                     out[place, pl.ds((t // ncol) * samples, samples), :] = mine
                 else:
@@ -117,23 +125,29 @@
     return rhs, diag
 
 
-def coupled(moved, where, r, ncol, share, samples, piece, kept=None, last=False):
+def coupled(moved, where, p, rows, ncol, share, samples, piece, kept=None):
     totals = [None] * piece
     pairs = samples // PAIR
     order = column_order(ncol)
+    step = stride(rows, ncol)
+    begin = step * (lax.axis_index("row") ^ p)
     for c in range(ncol):
+        if moved.shape[0] == ncol:
+            place = order.index(c)
+        else:
+            high, low = divmod(step * c % (rows * ncol), ncol)
+            place = ((begin + high) & (rows - 1)) * ncol + low
         for a in range(share):
-            place = r * ncol + c
+            keep = (p * ncol + c) * share + a
             if kept is not None:
                 first = a * (pairs + 1)
                 term = moved[place, pl.ds(first, pairs)].reshape(samples, moved.shape[3])
                 off = moved[place, first + pairs].astype(jnp.float32)[:1]
                 off = jnp.broadcast_to(off, term.shape)
-                kept[place * share + a] = off
+                kept[keep] = off
             else:
-                here = order.index(c) if last else place
-                term = moved[here, pl.ds(a * samples, samples), :]
-                off = where[place * share + a]
+                term = moved[place, pl.ds(a * samples, samples), :]
+                off = where[keep]
             term = term.astype(jnp.float32)
             for k in range(piece):
                 mine = jnp.where(off == k, term, 0.0)
@@ -165,10 +179,9 @@
         out, new_dir, new_res, new_sol, kept = refs[rows + 3 :]
     else:
         where, old_dir, old_res, old_sol, out, new_dir, new_res, new_sol = refs[rows + 3 :]
-    me = lax.axis_index("row")
     directions = []
     for p in range(rows):
-        image = coupled(moved, where, me ^ p, ncol, share, samples, piece, kept)
+        image = coupled(moved, where, p, rows, ncol, share, samples, piece, kept)
         for k in range(piece):
             rhs, diag = part(packed[p], k, width)
             inverse = 1.0 / diag
@@ -191,8 +204,7 @@
 def last_kernel(dims, share, packed, where, moved, old_dir, old_res, old_sol, solution, residual):
     rows, ncol, piece, width = dims
     samples = packed.shape[0] - 1
-    me = lax.axis_index("row")
-    image = coupled(moved, where, me, ncol, share, samples, piece, last=True)
+    image = coupled(moved, where, 0, rows, ncol, share, samples, piece)
     for k in range(piece):
         lanes = slice(k * width, (k + 1) * width)
         diag = packed[samples : samples + 1, lanes]
@@ -222,7 +234,12 @@
     params = pltpu.CompilerParams(vmem_limit_bytes=VMEM_BYTES)
 
     def exchange(x):
-        return lax.all_to_all(x, ("row", "col"), split_axis=0, concat_axis=0, tiled=True)
+        everyone = [0] * (rows * ncol)
+        for i in range(rows * ncol):
+            everyone[stride(rows, ncol) * i % (rows * ncol)] = i
+        return lax.all_to_all(
+            x, ("row", "col"), 0, 0, axis_index_groups=[everyone], tiled=True
+        )
 
     def exchange_columns(x):
         return lax.all_to_all(

time: 38.5 us -> 38.2 us (level)
  no operation moved by 1% of the time
where the time goes in v7:
time: 38.2 us; the launch traced here: 37.8 us
  blocking collectives  29 us (76%)
  starting transfers between devices  3.18 us (8%)
  Pallas kernels  2.95 us (8%)
  waiting for transfers between devices  1.43 us (4%)
  between operations  1.32 us (3%)
    all_to_all x2, blocking collectives, exchange(): lax.all_to_all(x, ('row', 'col'), 0, 0, axis_index_groups=[everyone], til...  20.8 us
    all_to_all x1, blocking collectives, exchange_columns(): lax.all_to_all(x, 'col', 0, 0, axis_index_groups=[column_order(ncol)], ti...  8.15 us
    ppermute x3, starting transfers between devices, body(): pieces[p] = lax.ppermute(packed, 'row', [(i, i ^ p) for i in range(rows)])  3.18 us
    ppermute x3, waiting for transfers between devices, body(): pieces[p] = lax.ppermute(packed, 'row', [(i, i ^ p) for i in range(rows)])  1.43 us
    pallas_call x1, Pallas kernels, body(): pl.pallas_call(functools.partial(prep_kernel, piece), out_shape=(grouped,...  0.97 us
  transfers between devices with their start and end apart: 3, of which 1 were waited for; matrix products, arithmetic and copies ran while one was open for 0% of the time, Pallas kernels for 3%

profile of v7, /device:TPU:0, one launch (start us, length us, event | category | flops | bytes accessed | tf_op | source)
XLA Modules:
  0.0 37.8 jit_solution(11549348806310084111)
XLA Ops:
  0.6 0.7 %shard_map.77.refs_0_.packed = f32[9,256]{1,0:T(8,128)S(1)} custom-call(f32[8,256]{1,0:T(8,128)} %rhs.1, f32[1,256]{1,0:T(1,128)} %bitcast.1), custom_call_target="tpu_custom_call" | custom-call | tf_op jit(solution)/shard_map/pallas_call | solution.py:252
  1.4 2.5 %collective-permute-start.2 = (f32[9,256]{1,0:T(8,128)S(1)}, f32[9,256]{1,0:T(8,128)S(1)}, u32[]{:S(2)}, u32[]{:S(2)}) collective-permute-start(f32[9,256]{1,0:T(8,128)S(1)} %shard_map.77.refs_0_.packed), channel_id=1, source_target_pairs={{0,24},{8,16},{16,8},{24,0},{1,25},{9,17},{17,9},{25,1},{2,26},{10... | collective-permute-start | bytes 27656 | tf_op jit(solution)/shard_map/ppermute | solution.py:279
  3.9 0.6 %collective-permute-start.1 = (f32[9,256]{1,0:T(8,128)S(1)}, f32[9,256]{1,0:T(8,128)S(1)}, u32[]{:S(2)}, u32[]{:S(2)}) collective-permute-start(f32[9,256]{1,0:T(8,128)S(1)} %shard_map.77.refs_0_.packed), channel_id=1, source_target_pairs={{0,16},{8,24},{16,0},{24,8},{1,17},{9,25},{17,1},{25,9},{2,18},{10... | collective-permute-start | bytes 27656 | tf_op jit(solution)/shard_map/ppermute | solution.py:279
  4.5 0.0 collective-permute-start
  5.2 1.0 %shard_map.78 = (bf16[4,128,256]{2,1,0:T(8,128)(2,1)S(1)}, s32[8,8,128]{2,1,0:T(8,128)S(1)}, s32[8,8,128]{2,1,0:T(8,128)S(1)}) custom-call(s32[1,1,8]{2,1,0:T(1,128)} %cols.1, s32[1,1,8]{2,1,0:T(1,128)} %offsets.1, s32[1,1,1]{2,1,0:T(1,128)S(6)} %copy.8.count, bf16[1,1,8,128,128]{4,3,2,1,0:T(8,128)(2,1)} %tiles.1), custom_call_target="tpu_custom_call" | custom-call | bytes 4194304 | tf_op jit(solution)/shard_map/pallas_call | solution.py:263
  6.2 0.0 collective-permute-done.2.refs_3_
  6.2 1.4 %collective-permute-done.1.refs_2_ = f32[9,256]{1,0:T(8,128)S(1)} collective-permute-done((f32[9,256]{1,0:T(8,128)S(1)}, f32[9,256]{1,0:T(8,128)S(1)}, u32[]{:S(2)}, u32[]{:S(2)}) %collective-permute-start.1) | collective-permute-done | bytes 9248 | tf_op jit(solution)/shard_map/ppermute | solution.py:279
  7.6 0.0 collective-permute-done.refs_1_
  7.6 0.2 shard_map.79
  7.8 11.9 %all_to_all.15.refs_6_ = bf16[32,5,2,128]{3,2,1,0:T(2,128)(2,1)S(1)} all-to-all(bf16[32,5,2,128]{3,2,1,0:T(2,128)(2,1)S(1)} %shard_map.79), channel_id=1, replica_groups={{0,27,22,17,12,7,2,29,24,19,14,9,4,31,26,21,16,11,6,1,28,23,18,13,8,3,3..., dimensions={0} | all-to-all | bytes 163840 | tf_op jit(solution)/shard_map/all_to_all | solution.py:240
  19.8 0.2 shard_map.80
  20.0 8.9 %all_to_all.16.refs_6_ = bf16[32,8,128]{2,1,0:T(8,128)(2,1)S(1)} all-to-all(bf16[32,8,128]{2,1,0:T(8,128)(2,1)S(1)} %get-tuple-element.18), channel_id=1, replica_groups={{0,27,22,17,12,7,2,29,24,19,14,9,4,31,26,21,16,11,6,1,28,23,18,13,8,3,3..., dimensions={0} | all-to-all | bytes 131072 | tf_op jit(solution)/shard_map/all_to_all | solution.py:240
  28.9 0.2 shard_map.81
  29.1 8.2 %all_to_all.17.moved = bf16[8,8,128]{2,1,0:T(8,128)(2,1)S(1)} all-to-all(bf16[8,8,128]{2,1,0:T(8,128)(2,1)S(1)} %get-tuple-element.22), channel_id=1, replica_groups={{3,2,1,0,7,6,5,4},{11,10,9,8,15,14,13,12},{19,18,17,16,23,22,21,20},{27..., dimensions={0} | all-to-all | bytes 32768 | tf_op jit(solution)/shard_map/all_to_all | solution.py:245
  37.2 0.6 %shard_map.82 = (f32[8,256]{1,0:T(8,128)}, f32[8,256]{1,0:T(8,128)}) custom-call(f32[9,256]{1,0:T(8,128)S(1)} %shard_map.77.refs_0_.packed, f32[32,8,128]{2,1,0:T(8,128)S(1)} %get-tuple-element.17.refs_7_.where, bf16[8,8,128]{2,1,0:T(8,128)(2,1)S(1)} %all_to_all.17.moved, f32[8,8,128]{2,1,0:T(8,128)S(1)} %get-tuple-element.23.old_dir, ...), custom_call_target="tpu_custom_call" | custom-call | tf_op jit(solution)/shard_map/pallas_call | solution.py:307
Async XLA Ops:
  1.4 4.8 %collective-permute-start.2 = (f32[9,256]{1,0:T(8,128)S(1)}, f32[9,256]{1,0:T(8,128)S(1)}, u32[]{:S(2)}, u32[]{:S(2)}) collective-permute-start(f32[9,256]{1,0:T(8,128)S(1)} %shard_map.77.refs_0_.packed), channel_id=1, source_target_pairs={{0,24},{8,16},{16,8},{24,0},{1,25},{9,17},{17,9},{25,1},{2,26},{10... | collective-permute-start | bytes 27656 | tf_op jit(solution)/shard_map/ppermute | solution.py:279
  3.9 3.7 %collective-permute-start.1 = (f32[9,256]{1,0:T(8,128)S(1)}, f32[9,256]{1,0:T(8,128)S(1)}, u32[]{:S(2)}, u32[]{:S(2)}) collective-permute-start(f32[9,256]{1,0:T(8,128)S(1)} %shard_map.77.refs_0_.packed), channel_id=1, source_target_pairs={{0,16},{8,24},{16,0},{24,8},{1,17},{9,25},{17,1},{25,9},{2,18},{10... | collective-permute-start | bytes 27656 | tf_op jit(solution)/shard_map/ppermute | solution.py:279
  4.5 3.1 %collective-permute-start = (f32[9,256]{1,0:T(8,128)S(1)}, f32[9,256]{1,0:T(8,128)S(1)}, u32[]{:S(2)}, u32[]{:S(2)}) collective-permute-start(f32[9,256]{1,0:T(8,128)S(1)} %shard_map.77.refs_0_.packed), channel_id=1, source_target_pairs={{0,8},{8,0},{16,24},{24,16},{1,9},{9,1},{17,25},{25,17},{2,10},{10... | collective-permute-start | bytes 27656 | tf_op jit(solution)/shard_map/ppermute | solution.py:279

commit v8 on v7

--- a/solution.py
+++ b/solution.py
@@ -70,9 +70,10 @@
         copy.wait()
 
 
-def stride(rows, ncol):
+def stride(rows, ncol, turn):
     n = rows * ncol
-    return n - 13 if n > 13 and math.gcd(n, 13) == 1 else 1
+    less = (5, 13)[turn]
+    return n - less if n > less and math.gcd(n, less) == 1 else 1
 
 
 def column_order(ncol):
@@ -83,6 +84,7 @@
 def multiply(directions, tiles, column, out, rows, ncol, offset=None):
     slots, samples, width = column.shape
     order = column_order(ncol)
+    step = stride(rows, ncol, 1 if offset is None else 0)
     blank = jnp.zeros((samples, width), jnp.bfloat16)
     for first in range(0, slots, GROUP):
         lines = []
@@ -104,7 +106,7 @@
             t = first + g
             mine = sent[g * samples : (g + 1) * samples].astype(jnp.bfloat16)
             for r in range(rows):
-                place = stride(rows, ncol) * (r * ncol + t % ncol) % (rows * ncol)
+                place = step * (r * ncol + t % ncol) % (rows * ncol)
                 if rows == 1:
                     place = order.index(t % ncol)
                 if offset is None:
@@ -129,7 +131,7 @@
     totals = [None] * piece
     pairs = samples // PAIR
     order = column_order(ncol)
-    step = stride(rows, ncol)
+    step = stride(rows, ncol, 1 if kept is None else 0)
     begin = step * (lax.axis_index("row") ^ p)
     for c in range(ncol):
         if moved.shape[0] == ncol:
@@ -194,9 +196,10 @@
                 direction, residual, total = old_dir[i], old_res[i], old_sol[i]
             residual = residual - (diag * direction + image[k])
             direction = a * direction + b * inverse * residual
-            new_dir[i] = direction
-            new_res[i] = residual
-            new_sol[i] = total + direction
+            if i < new_dir.shape[0]:
+                new_dir[i] = direction
+                new_res[i] = residual
+                new_sol[i] = total + direction
             directions.append(direction)
     multiply(directions, tiles, column, out, out.shape[0] // ncol, ncol)
 
@@ -225,6 +228,7 @@
     state = jax.ShapeDtypeStruct((blocks, samples, width), jnp.float32)
     grouped = jax.ShapeDtypeStruct((slots // GROUP, width, GROUP * width), tiles.dtype)
     kept = jax.ShapeDtypeStruct((rows * ncol * share, samples, width), jnp.float32)
+    own = jax.ShapeDtypeStruct((piece, samples, width), jnp.float32)
     table = jax.ShapeDtypeStruct((slots, samples, width), jnp.int32)
     narrow = jax.ShapeDtypeStruct((ncol, share * samples, width), jnp.bfloat16)
     message = jax.ShapeDtypeStruct((rows * ncol, share * samples, width), jnp.bfloat16)
@@ -233,10 +237,10 @@
     )
     params = pltpu.CompilerParams(vmem_limit_bytes=VMEM_BYTES)
 
-    def exchange(x):
+    def exchange(x, turn):
         everyone = [0] * (rows * ncol)
         for i in range(rows * ncol):
-            everyone[stride(rows, ncol) * i % (rows * ncol)] = i
+            everyone[stride(rows, ncol, turn) * i % (rows * ncol)] = i
         return lax.all_to_all(
             x, ("row", "col"), 0, 0, axis_index_groups=[everyone], tiled=True
         )
@@ -285,10 +289,12 @@
         out_specs=vmem,
         compiler_params=params,
     )(*pieces, held, column, offset)
-    moved = exchange(sent)
+    moved = exchange(sent, 0)
     states = []
     for step in range(STEPS - 1):
-        shapes = [message if step + 2 < STEPS else narrow, state, state, state]
+        shapes = [message, state, state, state]
+        if step + 2 == STEPS:
+            shapes = [narrow, own, own, own]
         if step == 0:
             shapes.append(kept)
         results = pl.pallas_call(
@@ -302,7 +308,7 @@
         if step == 0:
             where = results[4]
         states = [where, *results[1:4]]
-        moved = exchange(sent) if step + 2 < STEPS else exchange_columns(sent)
+        moved = exchange(sent, 1) if step + 2 < STEPS else exchange_columns(sent)
     out = jax.ShapeDtypeStruct(rhs.shape, jnp.float32)
     return pl.pallas_call(
         functools.partial(last_kernel, dims, share),

time: 38.2 us -> 38.2 us (level)
  no operation moved by 1% of the time
where the time goes in v8:
time: 38.2 us; the launch traced here: 37.9 us
  blocking collectives  29 us (76%)
  starting transfers between devices  3.18 us (8%)
  Pallas kernels  2.95 us (8%)
  waiting for transfers between devices  1.43 us (4%)
  between operations  1.32 us (3%)
    all_to_all x2, blocking collectives, exchange(): lax.all_to_all(x, ('row', 'col'), 0, 0, axis_index_groups=[everyone], til...  20.9 us
    all_to_all x1, blocking collectives, exchange_columns(): lax.all_to_all(x, 'col', 0, 0, axis_index_groups=[column_order(ncol)], ti...  8.15 us
    ppermute x3, starting transfers between devices, body(): pieces[p] = lax.ppermute(packed, 'row', [(i, i ^ p) for i in range(rows)])  3.18 us
    ppermute x3, waiting for transfers between devices, body(): pieces[p] = lax.ppermute(packed, 'row', [(i, i ^ p) for i in range(rows)])  1.43 us
    pallas_call x1, Pallas kernels, body(): pl.pallas_call(functools.partial(prep_kernel, piece), out_shape=(grouped,...  0.97 us
  transfers between devices with their start and end apart: 3, of which 1 were waited for; matrix products, arithmetic and copies ran while one was open for 0% of the time, Pallas kernels for 3%

profile of v8, /device:TPU:0, one launch (start us, length us, event | category | flops | bytes accessed | tf_op | source)
XLA Modules:
  0.0 37.9 jit_solution(7158975956133089208)
XLA Ops:
  0.6 0.7 %shard_map.77.refs_0_.packed = f32[9,256]{1,0:T(8,128)S(1)} custom-call(f32[8,256]{1,0:T(8,128)} %rhs.1, f32[1,256]{1,0:T(1,128)} %bitcast.1), custom_call_target="tpu_custom_call" | custom-call | tf_op jit(solution)/shard_map/pallas_call | solution.py:256
  1.4 2.5 %collective-permute-start.2 = (f32[9,256]{1,0:T(8,128)S(1)}, f32[9,256]{1,0:T(8,128)S(1)}, u32[]{:S(2)}, u32[]{:S(2)}) collective-permute-start(f32[9,256]{1,0:T(8,128)S(1)} %shard_map.77.refs_0_.packed), channel_id=1, source_target_pairs={{0,24},{8,16},{16,8},{24,0},{1,25},{9,17},{17,9},{25,1},{2,26},{10... | collective-permute-start | bytes 27656 | tf_op jit(solution)/shard_map/ppermute | solution.py:283
  3.9 0.6 %collective-permute-start.1 = (f32[9,256]{1,0:T(8,128)S(1)}, f32[9,256]{1,0:T(8,128)S(1)}, u32[]{:S(2)}, u32[]{:S(2)}) collective-permute-start(f32[9,256]{1,0:T(8,128)S(1)} %shard_map.77.refs_0_.packed), channel_id=1, source_target_pairs={{0,16},{8,24},{16,0},{24,8},{1,17},{9,25},{17,1},{25,9},{2,18},{10... | collective-permute-start | bytes 27656 | tf_op jit(solution)/shard_map/ppermute | solution.py:283
  4.5 0.0 collective-permute-start
  5.2 1.0 %shard_map.78 = (bf16[4,128,256]{2,1,0:T(8,128)(2,1)S(1)}, s32[8,8,128]{2,1,0:T(8,128)S(1)}, s32[8,8,128]{2,1,0:T(8,128)S(1)}) custom-call(s32[1,1,8]{2,1,0:T(1,128)} %cols.1, s32[1,1,8]{2,1,0:T(1,128)} %offsets.1, s32[1,1,1]{2,1,0:T(1,128)S(6)} %copy.8.count, bf16[1,1,8,128,128]{4,3,2,1,0:T(8,128)(2,1)} %tiles.1), custom_call_target="tpu_custom_call" | custom-call | bytes 4194304 | tf_op jit(solution)/shard_map/pallas_call | solution.py:267
  6.2 0.0 collective-permute-done.2.refs_3_
  6.2 1.4 %collective-permute-done.1.refs_2_ = f32[9,256]{1,0:T(8,128)S(1)} collective-permute-done((f32[9,256]{1,0:T(8,128)S(1)}, f32[9,256]{1,0:T(8,128)S(1)}, u32[]{:S(2)}, u32[]{:S(2)}) %collective-permute-start.1) | collective-permute-done | bytes 9248 | tf_op jit(solution)/shard_map/ppermute | solution.py:283
  7.6 0.0 collective-permute-done.refs_1_
  7.6 0.2 shard_map.79
  7.8 12.0 %all_to_all.15.refs_6_ = bf16[32,5,2,128]{3,2,1,0:T(2,128)(2,1)S(1)} all-to-all(bf16[32,5,2,128]{3,2,1,0:T(2,128)(2,1)S(1)} %shard_map.79), channel_id=1, replica_groups={{0,19,6,25,12,31,18,5,24,11,30,17,4,23,10,29,16,3,22,9,28,15,2,21,8,27,..., dimensions={0} | all-to-all | bytes 163840 | tf_op jit(solution)/shard_map/all_to_all | solution.py:244
  19.9 0.2 shard_map.80
  20.1 8.8 %all_to_all.16.refs_6_ = bf16[32,8,128]{2,1,0:T(8,128)(2,1)S(1)} all-to-all(bf16[32,8,128]{2,1,0:T(8,128)(2,1)S(1)} %get-tuple-element.18), channel_id=1, replica_groups={{0,27,22,17,12,7,2,29,24,19,14,9,4,31,26,21,16,11,6,1,28,23,18,13,8,3,3..., dimensions={0} | all-to-all | bytes 131072 | tf_op jit(solution)/shard_map/all_to_all | solution.py:244
  28.9 0.2 shard_map.81
  29.1 8.2 %all_to_all.17.moved = bf16[8,8,128]{2,1,0:T(8,128)(2,1)S(1)} all-to-all(bf16[8,8,128]{2,1,0:T(8,128)(2,1)S(1)} %get-tuple-element.22), channel_id=1, replica_groups={{3,2,1,0,7,6,5,4},{11,10,9,8,15,14,13,12},{19,18,17,16,23,22,21,20},{27..., dimensions={0} | all-to-all | bytes 32768 | tf_op jit(solution)/shard_map/all_to_all | solution.py:249
  37.3 0.6 %shard_map.82 = (f32[8,256]{1,0:T(8,128)}, f32[8,256]{1,0:T(8,128)}) custom-call(f32[9,256]{1,0:T(8,128)S(1)} %shard_map.77.refs_0_.packed, f32[32,8,128]{2,1,0:T(8,128)S(1)} %get-tuple-element.17.refs_7_.where, bf16[8,8,128]{2,1,0:T(8,128)(2,1)S(1)} %all_to_all.17.moved, f32[2,8,128]{2,1,0:T(8,128)S(1)} %get-tuple-element.23.old_dir, ...), custom_call_target="tpu_custom_call" | custom-call | tf_op jit(solution)/shard_map/pallas_call | solution.py:313
Async XLA Ops:
  1.4 4.8 %collective-permute-start.2 = (f32[9,256]{1,0:T(8,128)S(1)}, f32[9,256]{1,0:T(8,128)S(1)}, u32[]{:S(2)}, u32[]{:S(2)}) collective-permute-start(f32[9,256]{1,0:T(8,128)S(1)} %shard_map.77.refs_0_.packed), channel_id=1, source_target_pairs={{0,24},{8,16},{16,8},{24,0},{1,25},{9,17},{17,9},{25,1},{2,26},{10... | collective-permute-start | bytes 27656 | tf_op jit(solution)/shard_map/ppermute | solution.py:283
  3.9 3.7 %collective-permute-start.1 = (f32[9,256]{1,0:T(8,128)S(1)}, f32[9,256]{1,0:T(8,128)S(1)}, u32[]{:S(2)}, u32[]{:S(2)}) collective-permute-start(f32[9,256]{1,0:T(8,128)S(1)} %shard_map.77.refs_0_.packed), channel_id=1, source_target_pairs={{0,16},{8,24},{16,0},{24,8},{1,17},{9,25},{17,1},{25,9},{2,18},{10... | collective-permute-start | bytes 27656 | tf_op jit(solution)/shard_map/ppermute | solution.py:283
  4.5 3.1 %collective-permute-start = (f32[9,256]{1,0:T(8,128)S(1)}, f32[9,256]{1,0:T(8,128)S(1)}, u32[]{:S(2)}, u32[]{:S(2)}) collective-permute-start(f32[9,256]{1,0:T(8,128)S(1)} %shard_map.77.refs_0_.packed), channel_id=1, source_target_pairs={{0,8},{8,0},{16,24},{24,16},{1,9},{9,1},{17,25},{25,17},{2,10},{10... | collective-permute-start | bytes 27656 | tf_op jit(solution)/shard_map/ppermute | solution.py:283
